TPU v7x, 512 devices: a whole 4x8x8 slice. The times are simulated.
512 devices in a mesh: blk: 32 (over y, x), head: 16 (over z, core).
Axes of the slice: x: 4, y: 8, z: 8, core: 2. Of those that a mesh axis runs over, the one named last changes fastest.
Arguments:
- tokens: bfloat16 [2048, 4096], P('blk', 'head'), may hold values from -6 to 6
- queries: bfloat16 [2048, 36864], P('blk', 'head'), may hold values from -600 to 600
- latents: bfloat16 [2048, 576], P('blk'), may hold values from -6 to 6
- value_up: bfloat16 [64, 512, 128], P('head'), may hold values from -0.25 to 0.25
- out_proj: bfloat16 [8192, 4096], P('head', 'blk'), may hold values from -0.09375 to 0.09375
- expert_ids: int32 [2048, 8], P('blk'), may hold values from 0 to 31, all different within a row; in each aligned block of 64 rows (0 to 63, 64 to 127, ...) at most 20 rows name the same one
- expert_gates: float32 [2048, 8], P('blk'), may hold values from 0.05 to 0.5
- w_gate: bfloat16 [32, 4096, 2048], P('blk', None, 'head'), may hold values from -0.09375 to 0.09375
- w_up: bfloat16 [32, 4096, 2048], P('blk', None, 'head'), may hold values from -0.09375 to 0.09375
- w_down: bfloat16 [32, 2048, 4096], P('blk', None, 'head'), may hold values from -0.125 to 0.125
Outputs:
- result: bfloat16 [2048, 4096], P('blk', 'head')
Inputs may be any that keep to these rules, and one draw needn't show every extreme that they name: `expert_ids`: among the tokens of one index of blk (aligned blocks of 64 rows) at most 20 choose one expert, and some expert is chosen by exactly 20 of them; the experts of one row differ.
All inputs are finite; a program needn't handle non-finite values.
Results may differ from a plain program's by a relative error of at most 0.013.
Values may be sent and summed in bfloat16 or wider, within the bound.
No kernel may reach another device: no remote copies, remote signals or barrier semaphores. Data moves between devices by JAX's collectives and lax.ppermute only.
A program may use at most 64 MiB of HBM per device.

v0:
```python
import jax
import jax.numpy as jnp
from jax import lax
from jax.sharding import PartitionSpec as P

D = 4096
LAT = 512
ROPE = 64
QKNOPE = 128
EXPERTS = 32
CAP = 20


def per_device(
    tokens, queries, latents, value_up, out_proj, expert_ids, expert_gates, w_gate, w_up, w_down
):
    row_count = tokens.shape[0]
    heads_here = value_up.shape[0]
    first_row = lax.axis_index("blk") * row_count
    score_scale = (QKNOPE + ROPE) ** (-0.5)
    query_heads = queries.reshape(row_count, heads_here, LAT + ROPE)
    query_pos = first_row + jnp.arange(row_count, dtype=jnp.int32)
    last_query = first_row + row_count - 1
    start_state = (
        jnp.full((row_count, heads_here), -1e30, jnp.float32),
        jnp.zeros((row_count, heads_here), jnp.float32),
        jnp.zeros((row_count, heads_here, LAT), jnp.float32),
    )
    segment = lax.all_gather(latents, "blk", axis=0, tiled=True)

    def compute(state_in):
        running_max, denominator, accumulated = state_in
        key_count = segment.shape[0]
        scores = (
            jnp.einsum("qhc,kc->qhk", query_heads, segment, preferred_element_type=jnp.float32)
            * score_scale
        )
        key_pos = jnp.arange(key_count, dtype=jnp.int32)
        allowed = (key_pos[None, :] <= query_pos[:, None])[:, None, :]
        scores = jnp.where(allowed, scores, -1e30)
        new_max = jnp.maximum(running_max, jnp.max(scores, axis=2))
        exp_weights = jnp.where(allowed, jnp.exp(scores - new_max[:, :, None]), 0.0)
        denominator = jnp.sum(exp_weights, axis=2)
        accumulated = jnp.einsum(
            "qhk,kc->qhc",
            exp_weights.astype(jnp.bfloat16),
            segment[:, :LAT],
            preferred_element_type=jnp.float32,
        )
        return (new_max, denominator, accumulated)

    def keep(state_in):
        return state_in

    running_max, denominator, accumulated = lax.cond(
        jnp.int32(0) <= last_query, compute, keep, start_state
    )
    context = (accumulated / denominator[:, :, None]).astype(jnp.bfloat16)
    lifted = jnp.einsum(
        "qhc,hcv->qhv", context, value_up, preferred_element_type=jnp.float32
    ).astype(jnp.bfloat16)
    lifted = lifted.reshape(row_count, heads_here * value_up.shape[2])
    partial_out = jnp.dot(
        lifted,
        lax.all_gather(out_proj, "blk", axis=1, tiled=True),
        preferred_element_type=jnp.float32,
    )
    attended = lax.psum_scatter(
        partial_out.astype(jnp.bfloat16), "head", scatter_dimension=1, tiled=True
    ).astype(jnp.float32)
    mid_state = (tokens.astype(jnp.float32) + attended).astype(jnp.bfloat16)
    mid_wide = mid_state.astype(jnp.float32)
    squares = lax.psum(jnp.sum(mid_wide * mid_wide, axis=1), "head")
    normed = (mid_wide * lax.rsqrt(squares / D + 1e-06)[:, None]).astype(jnp.bfloat16)
    flat_ids = expert_ids.reshape(-1)
    choose_count = expert_ids.shape[1]
    onehot_ids = (flat_ids[:, None] == jnp.arange(EXPERTS, dtype=jnp.int32)[None, :]).astype(
        jnp.int32
    )
    earlier = jnp.cumsum(onehot_ids, axis=0) - onehot_ids
    ranks = jnp.sum(earlier * onehot_ids, axis=1)
    slot_ids = flat_ids * CAP + ranks
    slot_hits = jnp.arange(EXPERTS * CAP, dtype=jnp.int32)[:, None] == slot_ids[None, :]
    select = jnp.sum(
        slot_hits.astype(jnp.bfloat16).reshape(EXPERTS * CAP, row_count, choose_count), axis=2
    )
    combine = jnp.sum(
        jnp.where(slot_hits, expert_gates.reshape(-1)[None, :], 0.0).reshape(
            EXPERTS * CAP, row_count, choose_count
        ),
        axis=2,
    )
    outgoing = (
        jnp.dot(select, normed, preferred_element_type=jnp.float32)
        .astype(jnp.bfloat16)
        .reshape(EXPERTS, CAP, normed.shape[1])
    )
    incoming = lax.all_to_all(outgoing, "blk", split_axis=0, concat_axis=1, tiled=True)
    contract_segment = lax.all_gather(incoming, "head", axis=2, tiled=True)
    gate_add = jnp.einsum(
        "esd,edf->esf", contract_segment, w_gate, preferred_element_type=jnp.float32
    )
    up_add = jnp.einsum("esd,edf->esf", contract_segment, w_up, preferred_element_type=jnp.float32)
    activation = (jax.nn.silu(gate_add) * up_add).astype(jnp.bfloat16)
    expert_out = jnp.einsum(
        "esf,efd->esd",
        lax.all_gather(activation, "head", axis=2, tiled=True),
        w_down,
        preferred_element_type=jnp.float32,
    ).astype(jnp.bfloat16)
    returned = lax.all_to_all(expert_out, "blk", split_axis=1, concat_axis=0, tiled=True)
    returned_wide = returned.reshape(EXPERTS * CAP, returned.shape[2]).astype(jnp.float32)
    routed = jnp.einsum("sr,sd->rd", combine, returned_wide, precision=lax.Precision.HIGHEST)
    return (mid_wide + routed).astype(jnp.bfloat16)


def solution(mesh):
    placed = (
        P("blk", "head"),
        P("blk", "head"),
        P("blk", None),
        P("head", None, None),
        P("head", "blk"),
        P("blk", None),
        P("blk", None),
        P("blk", None, "head"),
        P("blk", None, "head"),
        P("blk", None, "head"),
    )
    return jax.shard_map(
        per_device, mesh=mesh, in_specs=placed, out_specs=P("blk", "head"), check_vma=False
    )
```

profile of v0, /device:TPU:8, one launch (start us, length us, event | category | flops | bytes accessed | tf_op | source)
XLA Modules:
  0.0 443.7 jit_solution(13091606071966224623)
XLA Ops:
  8.1 90.0 %all-gather.6.cloned.1.call-done = bf16[2048,576]{1,0:T(8,128)(2,1)} async-done(((bf16[64,576]{1,0:T(8,128)(2,1)}), bf16[2048,576]{1,0:T(8,128)(2,1)}) %all-gather.6.cloned.1.call-update) | async-done | bytes 2359312 | tf_op jit(solution)/shard_map/all_gather | solution.py:29
  98.1 6.0 %conditional.1 = (f32[64,4]{0,1:T(4,128)S(1)}, f32[64,4,512]{2,0,1:T(8,128)S(1)}) conditional(s32[]{:T(128)} %convert_element_type.66, () %tuple.13, (s32[]{:T(128)}, s32[64]{0:T(128)S(1)}, bf16[64,2304]{1,0:T(8,128)(2,1)}, bf16[2048,576]{1,0:T(8,128)(2,1)}) %tuple.14), branch_computations={%region_0.0_spmd, %region_1.4_spmd} | conditional | flops 1145700096 | bytes 22126384 | solution.py:55
  98.2 1.4 reshape.109
  99.6 3.1 fusion.44
  102.7 0.8 fusion.2
  104.3 83.3 %all-gather.8.cloned.1.call-done = bf16[512,4096]{1,0:T(8,128)(2,1)} async-done(((bf16[512,128]{1,0:T(8,128)(2,1)}), bf16[512,4096]{1,0:T(8,128)(2,1)}) %all-gather.8.cloned.1.call-update) | async-done | bytes 4194320 | tf_op jit(solution)/shard_map/all_gather | solution.py:65
  187.6 3.8 convolution_convert_fusion
  191.9 1.2 reduce-window.6
  194.1 58.6 %reduce-scatter.2.cloned.1.call-done = bf16[64,256]{1,0:T(8,128)(2,1)} async-done(((bf16[64,4096]{1,0:T(8,128)(2,1)}), bf16[64,256]{1,0:T(8,128)(2,1)}) %reduce-scatter.2.cloned.1.call-update) | async-done | bytes 32784 | tf_op jit(solution)/shard_map/reduce_scatter | solution.py:68
  252.7 0.9 fusion.34
  253.6 23.6 %psum.7 = f32[64]{0:T(128)S(1)} all-reduce(f32[64]{0:T(128)S(1)} %fusion.34), channel_id=1, replica_groups=mesh['blk'=32,'head'=16] {'head'}, use_global_device_ids=true, to_apply=%region_11.12 | all-reduce | flops 64 | bytes 512 | tf_op jit(solution)/shard_map/psum | solution.py:73
  277.2 1.1 convolution_convert_fusion.2
  278.3 24.3 %all_to_all.21 = bf16[32,20,256]{2,1,0:T(8,128)(2,1)S(1)} all-to-all(bf16[32,20,256]{2,1,0:T(8,128)(2,1)S(1)} %reshape.121), channel_id=1, replica_groups=mesh['blk'=32,'head'=16] {'blk'}, dimensions={0} | all-to-all | bytes 655360 | tf_op jit(solution)/shard_map/all_to_all | solution.py:98
  302.7 0.8 all_to_all.7
  303.6 49.1 %all-gather.10.cloned.1.call-done = bf16[1,640,4096]{2,1,0:T(8,128)(2,1)} async-done(((bf16[1,640,256]{2,1,0:T(8,128)(2,1)}), bf16[1,640,4096]{2,1,0:T(8,128)(2,1)}) %all-gather.10.cloned.1.call-update) | async-done | bytes 5242896 | tf_op jit(solution)/shard_map/all_gather | solution.py:99
  352.6 4.1 fusion.15
  356.8 3.4 fusion.22
  360.2 45.0 %all-gather.12.cloned.1.call-done = bf16[640,2048]{1,0:T(8,128)(2,1)} async-done(((bf16[640,128]{1,0:T(8,128)(2,1)}), bf16[640,2048]{1,0:T(8,128)(2,1)}) %all-gather.12.cloned.1.call-update) | async-done | bytes 2621456 | tf_op jit(solution)/shard_map/all_gather | solution.py:107
  405.3 2.6 fusion.18
  408.9 2.7 reduce.3
  411.6 0.8 reshape.133
  412.4 9.8 %all-to-all-start.1 = ((bf16[32,2,2560]{2,1,0:T(2,128)(2,1)}), bf16[32,2,2560]{2,1,0:T(2,128)(2,1)S(1)}, u32[]{:S(2)}, u32[]{:S(2)}) async-start(bf16[32,2,2560]{2,1,0:T(2,128)(2,1)} %reshape.133), calls=%async_computation.2 | async-start | bytes 655360 | tf_op jit(solution)/shard_map/all_to_all | solution.py:111
  422.8 13.2 %all-to-all-done.1 = bf16[32,2,2560]{2,1,0:T(2,128)(2,1)S(1)} async-done(((bf16[32,2,2560]{2,1,0:T(2,128)(2,1)}), bf16[32,2,2560]{2,1,0:T(2,128)(2,1)S(1)}, u32[]{:S(2)}, u32[]{:S(2)}) %all-to-all-start.1) | async-done | bytes 327712 | tf_op jit(solution)/shard_map/all_to_all | solution.py:111
  436.3 0.9 fusion.26
  (54 shorter events, 5.9 us)
Async XLA Ops:
  6.5 398.7 %copy-start = (bf16[1,2048,256]{2,1,0:T(8,128)(2,1)S(1)}, bf16[1,2048,256]{2,1,0:T(8,128)(2,1)}, u32[]{:S(2)}) copy-start(bf16[1,2048,256]{2,1,0:T(8,128)(2,1)} %param.21) | copy-start | bytes 3145732
  6.5 91.5 %all-gather.6.cloned.1.call-start = ((), (), s32[]{:S(2)}) async-start(), calls=%async_computation.3 | async-start | bytes 2703360 | tf_op jit(solution)/shard_map/all_gather | solution.py:29
  7.3 180.4 %all-gather.8.cloned.1.call-start = ((), (), s32[]{:S(2)}) async-start(), calls=%async_computation.4 | async-start | bytes 4325376 | tf_op jit(solution)/shard_map/all_gather | solution.py:65
  8.0 244.7 %reduce-scatter.2.cloned.1.call-start = ((), (), s32[]{:S(2)}) async-start(), calls=%async_computation.5 | async-start | bytes 557056 | tf_op jit(solution)/shard_map/reduce_scatter | solution.py:68
  98.1 6.0 %copy-start.8 = (bf16[4,512,128]{2,1,0:T(8,128)(2,1)S(1)}, bf16[4,512,128]{2,1,0:T(8,128)(2,1)}, u32[]{:S(2)}) copy-start(bf16[4,512,128]{2,1,0:T(8,128)(2,1)} %param.15) | copy-start | bytes 1572868
  99.6 3.1 copy-start.6
  104.3 87.3 %copy-start.3 = (s32[64,8]{0,1:T(8,128)S(1)}, s32[64,8]{0,1:T(8,128)}, u32[]{:S(2)}) copy-start(s32[64,8]{0,1:T(8,128)} %param.17) | copy-start | bytes 6148
  104.3 148.4 %copy-start.1 = (bf16[64,256]{1,0:T(8,128)(2,1)S(1)}, bf16[64,256]{1,0:T(8,128)(2,1)}, u32[]{:S(2)}) copy-start(bf16[64,256]{1,0:T(8,128)(2,1)} %param.12) | copy-start | bytes 98308
  191.5 161.1 %copy-start.7 = (bf16[1,4096,128]{2,1,0:T(8,128)(2,1)S(1)}, bf16[1,4096,128]{2,1,0:T(8,128)(2,1)}, u32[]{:S(2)}) copy-start(bf16[1,4096,128]{2,1,0:T(8,128)(2,1)} %param.19) | copy-start | bytes 3145732
  191.5 161.1 %all-gather.10.cloned.1.call-start = ((), (), s32[]{:S(2)}) async-start(), calls=%async_computation.6 | async-start | bytes 5570560 | tf_op jit(solution)/shard_map/all_gather | solution.py:99
  303.5 101.7 %all-gather.12.cloned.1.call-start = ((), (), s32[]{:S(2)}) async-start(), calls=%async_computation.7 | async-start | bytes 2785280 | tf_op jit(solution)/shard_map/all_gather | solution.py:107
  352.6 4.1 copy-start.5
  407.8 14.4 %copy-start.4 = (f32[64,8]{0,1:T(8,128)S(1)}, f32[64,8]{0,1:T(8,128)}, u32[]{:S(2)}) copy-start(f32[64,8]{0,1:T(8,128)} %param.18) | copy-start | bytes 6148
  407.9 28.5 %copy-start.2 = (bf16[64,256]{1,0:T(8,128)(2,1)S(1)}, bf16[64,256]{1,0:T(8,128)(2,1)}, u32[]{:S(2)}) copy-start(bf16[64,256]{1,0:T(8,128)(2,1)} %reduce-scatter.2.cloned.1.call-done) | copy-start | bytes 98308
  412.4 23.6 %all-to-all-start.1 = ((bf16[32,2,2560]{2,1,0:T(2,128)(2,1)}), bf16[32,2,2560]{2,1,0:T(2,128)(2,1)S(1)}, u32[]{:S(2)}, u32[]{:S(2)}) async-start(bf16[32,2,2560]{2,1,0:T(2,128)(2,1)} %reshape.133), calls=%async_computation.2 | async-start | bytes 655360 | tf_op jit(solution)/shard_map/all_to_all | solution.py:111
Sparse Core Ops, SparseCore 0:
  10.5 87.5 all-gather.5
  101.1 86.5 all-gather.7
  191.6 61.0 reduce-scatter.1
  303.6 48.9 all-gather.9
  360.3 44.8 all-gather.11
where the time goes:
time: 444 us
  waiting for transfers between devices  341 us (77%)
  blocking collectives  47.9 us (11%)
  matrix products  20.1 us (5%)
  between operations  13.3 us (3%)
  starting transfers between devices  10 us (2%)
  other arithmetic  6.52 us (1%)
  local copies, waits for them, and re-layouts  5.17 us (1%)
    all_gather x1, waiting for transfers between devices, per_device(): segment = lax.all_gather(latents, 'blk', axis=0, tiled=True)  90 us
    all_gather x1, waiting for transfers between devices, per_device(): lax.all_gather(out_proj, 'blk', axis=1, tiled=True)  83.3 us
    reduce_scatter x1, waiting for transfers between devices, per_device(): lax.psum_scatter(partial_out.astype(jnp.bfloat16), 'head', scatter_dimens...  58.6 us
    all_gather x1, waiting for transfers between devices, per_device(): contract_segment = lax.all_gather(incoming, 'head', axis=2, tiled=True)  49.1 us
    all_gather x1, waiting for transfers between devices, per_device(): lax.all_gather(activation, 'head', axis=2, tiled=True)  45 us
    all_to_all x1, blocking collectives, per_device(): lax.all_to_all(outgoing, 'blk', split_axis=0, concat_axis=1, tiled=True)  24.3 us
    psum x1, blocking collectives, per_device(): squares = lax.psum(jnp.sum(mid_wide * mid_wide, axis=1), 'head')  23.6 us
    all_to_all x1, waiting for transfers between devices, per_device(): lax.all_to_all(expert_out, 'blk', split_axis=1, concat_axis=0, tiled=True)  13.2 us
  transfers between devices with their start and end apart: 6, of which 6 were waited for; matrix products, arithmetic and copies ran while one was open for 2% of the time, Pallas kernels for 0%

commit v1 on v0

v1 whole, which is shorter than its diff:
```python
import functools

import jax
import jax.numpy as jnp
from jax import lax
from jax.experimental import pallas as pl
from jax.experimental.pallas import tpu as pltpu
from jax.sharding import PartitionSpec as P

D = 4096
LAT = 512
ROPE = 64
QKNOPE = 128
VDIM = 128
EXPERTS = 32
CAP = 20
SLOTS = EXPERTS * CAP
TOK = 64
HALF = TOK // 2
N_BLK = 32
N_HEAD = 16
N_X = 4
N_Y = 8
HEADS_HERE = 4
KEYS = N_BLK * HALF
SCALE = (QKNOPE + ROPE) ** (-0.5)

X_GROUPS = [[y * N_X + x for x in range(N_X)] for y in range(N_Y)]
Y_GROUPS = [[y * N_X + x for y in range(N_Y)] for x in range(N_X)]
XH_GROUPS = [[y * 64 + i for i in range(64)] for y in range(N_Y)]
CORE_SWAP = [(i, i ^ 1) for i in range(N_HEAD)]


def attention_kernel(place_ref, q_ref, own_ref, other_ref, lift_ref, out_ref):
    width = LAT + ROPE
    q_all = q_ref[...]
    q_rows = jnp.concatenate(
        [q_all[:, h * width : (h + 1) * width] for h in range(HEADS_HERE)], axis=0
    )
    rows = HEADS_HERE * TOK
    first = place_ref[0] * TOK
    core = place_ref[1]
    query_pos = first + (lax.broadcasted_iota(jnp.int32, (rows, KEYS), 0) & (TOK - 1))
    key_idx = lax.broadcasted_iota(jnp.int32, (rows, KEYS), 1)
    key_base = (key_idx >> 5) * TOK + (key_idx & (HALF - 1))
    scores, maxes, masks = [], [], []
    for part, ref in ((core, own_ref), (1 - core, other_ref)):
        raw = lax.dot_general(
            q_rows, ref[...], (((1,), (1,)), ((), ())), preferred_element_type=jnp.float32
        )
        allowed = key_base + part * HALF <= query_pos
        raw = jnp.where(allowed, raw * SCALE, -1e30)
        scores.append(raw)
        masks.append(allowed)
        maxes.append(jnp.max(raw, axis=1, keepdims=True))
    row_max = jnp.maximum(maxes[0], maxes[1])
    denominator = 0.0
    context = 0.0
    for raw, allowed, ref in zip(scores, masks, (own_ref, other_ref)):
        weights = jnp.where(allowed, jnp.exp(raw - row_max), 0.0)
        denominator = denominator + jnp.sum(weights, axis=1, keepdims=True)
        context = context + jnp.dot(
            weights.astype(jnp.bfloat16), ref[:, :LAT], preferred_element_type=jnp.float32
        )
    context = (context / denominator).astype(jnp.bfloat16)
    for h in range(HEADS_HERE):
        out_ref[:, h * VDIM : (h + 1) * VDIM] = jnp.dot(
            context[h * TOK : (h + 1) * TOK], lift_ref[h], preferred_element_type=jnp.float32
        ).astype(jnp.bfloat16)


def project_kernel(lifted_ref, proj_ref, out_ref):
    lifted = lifted_ref[...]
    for pair in range(N_Y // 2):
        weights = jnp.concatenate([proj_ref[2 * pair], proj_ref[2 * pair + 1]], axis=1)
        full = jnp.dot(lifted, weights, preferred_element_type=jnp.float32).astype(jnp.bfloat16)
        for side in range(2):
            for x in range(N_X):
                for p in range(2):
                    row = x * TOK + p * HALF
                    out_ref[x * 16 + (2 * pair + side) * 2 + p] = full[
                        row : row + HALF, side * 128 : (side + 1) * 128
                    ]


def hidden_kernel(steps, rows_ref, gate_ref, up_ref, out_ref, acc_ref, square_ref):
    step = pl.program_id(0)

    @pl.when(step == 0)
    def _():
        acc_ref[...] = jnp.zeros_like(acc_ref)
        square_ref[...] = jnp.zeros_like(square_ref)

    total = acc_ref[...]
    squares = square_ref[...]
    for i in range(rows_ref.shape[0]):
        rows = rows_ref[i]
        weights = jnp.concatenate(
            [gate_ref[i * 256 : (i + 1) * 256], up_ref[i * 256 : (i + 1) * 256]], axis=1
        )
        total = total + jnp.dot(rows, weights, preferred_element_type=jnp.float32)
        wide = rows.astype(jnp.float32)
        wide = wide * wide
        squares = squares + (wide[:, :128] + wide[:, 128:])
    acc_ref[...] = total
    square_ref[...] = squares

    @pl.when(step == steps - 1)
    def _():
        mean = jnp.sum(square_ref[...], axis=1, keepdims=True) / D
        inverse = lax.rsqrt(mean + 1e-06)
        gate = acc_ref[:, :128] * inverse
        up = acc_ref[:, 128:] * inverse
        out_ref[...] = (gate / (1.0 + jnp.exp(-gate)) * up).astype(jnp.bfloat16)


def down_kernel(steps, act_ref, down_ref, out_ref, acc_ref):
    step = pl.program_id(0)

    @pl.when(step == 0)
    def _():
        acc_ref[...] = jnp.zeros_like(acc_ref)

    parts = act_ref.shape[0]
    wide = jnp.concatenate([act_ref[i] for i in range(parts)], axis=1)
    acc_ref[...] += jnp.dot(wide, down_ref[...], preferred_element_type=jnp.float32)

    @pl.when(step == steps - 1)
    def _():
        out_ref[...] = acc_ref[...].astype(jnp.bfloat16)


def attend(place, queries, own, other, value_up):
    return pl.pallas_call(
        attention_kernel,
        out_shape=jax.ShapeDtypeStruct((TOK, HEADS_HERE * VDIM), jnp.bfloat16),
        in_specs=[pl.BlockSpec(memory_space=pltpu.SMEM)]
        + [pl.BlockSpec(memory_space=pltpu.VMEM)] * 4,
        out_specs=pl.BlockSpec(memory_space=pltpu.VMEM),
        name="attend",
    )(place, queries, own, other, value_up)


def project(lifted, proj):
    return pl.pallas_call(
        project_kernel,
        out_shape=jax.ShapeDtypeStruct((64, HALF, 128), jnp.bfloat16),
        name="project",
    )(lifted, proj)


def hidden(rows, w_gate, w_up):
    steps = 4
    per = N_HEAD // steps
    return pl.pallas_call(
        functools.partial(hidden_kernel, steps),
        out_shape=jax.ShapeDtypeStruct((SLOTS, 128), jnp.bfloat16),
        grid=(steps,),
        in_specs=[
            pl.BlockSpec((per, SLOTS, 256), lambda i: (i, 0, 0)),
            pl.BlockSpec((per * 256, 128), lambda i: (i, 0)),
            pl.BlockSpec((per * 256, 128), lambda i: (i, 0)),
        ],
        out_specs=pl.BlockSpec((SLOTS, 128), lambda i: (0, 0)),
        scratch_shapes=[
            pltpu.VMEM((SLOTS, 256), jnp.float32),
            pltpu.VMEM((SLOTS, 128), jnp.float32),
        ],
        name="hidden",
    )(rows, w_gate, w_up)


def down(act, w_down):
    steps = 2
    per = N_HEAD // steps
    return pl.pallas_call(
        functools.partial(down_kernel, steps),
        out_shape=jax.ShapeDtypeStruct((SLOTS, 256), jnp.bfloat16),
        grid=(steps,),
        in_specs=[
            pl.BlockSpec((per, SLOTS, 128), lambda i: (i, 0, 0)),
            pl.BlockSpec((per * 128, 256), lambda i: (i, 0)),
        ],
        out_specs=pl.BlockSpec((SLOTS, 256), lambda i: (0, 0)),
        scratch_shapes=[pltpu.VMEM((SLOTS, 256), jnp.float32)],
        name="down",
    )(act, w_down)


def per_device(
    tokens, queries, latents, value_up, out_proj, expert_ids, expert_gates, w_gate, w_up, w_down
):
    blk = lax.axis_index("blk")
    core = lax.axis_index("head") & 1

    half = lax.dynamic_slice(latents, (core * HALF, 0), (HALF, LAT + ROPE))
    own = lax.all_to_all(
        jnp.broadcast_to(half[None], (N_BLK,) + half.shape), "blk", 0, 0, tiled=True
    ).reshape(KEYS, LAT + ROPE)
    other = lax.ppermute(own, "head", CORE_SWAP)

    proj = lax.all_gather(
        out_proj, "blk", axis=0, tiled=True, axis_index_groups=Y_GROUPS
    ).reshape(N_Y, out_proj.shape[0], 128)

    place = jnp.stack([blk, core]).astype(jnp.int32)
    lifted = attend(place, queries, own, other, value_up)

    lifted_row = lax.all_to_all(
        jnp.broadcast_to(lifted[None], (N_X,) + lifted.shape),
        "blk",
        0,
        0,
        tiled=True,
        axis_index_groups=X_GROUPS,
    ).reshape(N_X * TOK, lifted.shape[1])
    partial = project(lifted_row, proj)
    spread = lax.all_to_all(
        partial, ("blk", "head"), 0, 0, tiled=True, axis_index_groups=XH_GROUPS
    )
    summed = jnp.sum(spread.reshape(N_X, N_HEAD, HALF, 128).astype(jnp.float32), axis=1)
    keep = lax.dynamic_slice(summed, (2 * core, 0, 0), (2, HALF, 128))
    send = lax.dynamic_slice(summed, (2 - 2 * core, 0, 0), (2, HALF, 128))
    got = lax.ppermute(send, "head", CORE_SWAP)
    top = jnp.where(core == 0, keep, got)
    bottom = jnp.where(core == 0, got, keep)
    attended = jnp.concatenate([top, bottom], axis=1)
    attended = jnp.concatenate([attended[0], attended[1]], axis=1)
    mid_state = (tokens.astype(jnp.float32) + attended).astype(jnp.bfloat16)
    mid_wide = mid_state.astype(jnp.float32)

    row_count = tokens.shape[0]
    flat_ids = expert_ids.reshape(-1)
    choose_count = expert_ids.shape[1]
    onehot_ids = (flat_ids[:, None] == jnp.arange(EXPERTS, dtype=jnp.int32)[None, :]).astype(
        jnp.int32
    )
    earlier = jnp.cumsum(onehot_ids, axis=0) - onehot_ids
    ranks = jnp.sum(earlier * onehot_ids, axis=1)
    slot_ids = flat_ids * CAP + ranks
    slot_hits = jnp.arange(SLOTS, dtype=jnp.int32)[:, None] == slot_ids[None, :]
    select = jnp.sum(
        slot_hits.astype(jnp.bfloat16).reshape(SLOTS, row_count, choose_count), axis=2
    )
    combine = jnp.sum(
        jnp.where(slot_hits, expert_gates.reshape(-1)[None, :], 0.0).reshape(
            SLOTS, row_count, choose_count
        ),
        axis=2,
    )

    outgoing = (
        jnp.dot(select, mid_state, preferred_element_type=jnp.float32)
        .astype(jnp.bfloat16)
        .reshape(EXPERTS, CAP, 256)
    )
    incoming = lax.all_to_all(outgoing, "blk", split_axis=0, concat_axis=0, tiled=True)
    rows = lax.all_gather(incoming.reshape(SLOTS, 256), "head", axis=0, tiled=True)
    act = hidden(rows.reshape(N_HEAD, SLOTS, 256), w_gate[0], w_up[0])
    acts = lax.all_gather(act, "head", axis=0, tiled=True)
    expert_out = down(acts.reshape(N_HEAD, SLOTS, 128), w_down[0])
    returned = lax.all_to_all(
        expert_out.reshape(EXPERTS, CAP, 256), "blk", split_axis=0, concat_axis=0, tiled=True
    )
    returned_wide = returned.reshape(SLOTS, 256).astype(jnp.float32)
    routed = jnp.einsum("sr,sd->rd", combine, returned_wide, precision=lax.Precision.HIGHEST)
    return (mid_wide + routed).astype(jnp.bfloat16)


def solution(mesh):
    placed = (
        P("blk", "head"),
        P("blk", "head"),
        P("blk", None),
        P("head", None, None),
        P("head", "blk"),
        P("blk", None),
        P("blk", None),
        P("blk", None, "head"),
        P("blk", None, "head"),
        P("blk", None, "head"),
    )
    return jax.shard_map(
        per_device, mesh=mesh, in_specs=placed, out_specs=P("blk", "head"), check_vma=False
    )
```

time: 444 us -> 265 us (0.60)
  waiting for transfers between devices: 341 us -> 156 us
  starting transfers between devices: 10 us -> 42.8 us
  blocking collectives: 47.9 us -> 21.8 us
  matrix products: 20.1 us -> 1.17 us
  Pallas kernels: 0 us -> 16.2 us
  local copies, waits for them, and re-layouts: 5.17 us -> 10.9 us
    all_gather x4 -> x3, waiting for transfers between devices: 267 us -> 80.2 us  [the longest x1 41.7 us: per_device(): acts = lax.all_gather(act, 'head', axis=0, tiled=True)]
    reduce_scatter x1 -> x0, waiting for transfers between devices: 58.6 us -> none  [per_device(): lax.psum_scatter(partial_out.astype(jnp.bfloat16), 'head', scatter_dimens...]
    all_to_all x1 -> x4, waiting for transfers between devices: 13.2 us -> 71.8 us  [the longest x1 35.4 us: per_device(): lax.all_to_all(jnp.broadcast_to(half[None], (N_BLK,) + half.shape), 'blk'...]
    all_to_all x1 -> x4, starting transfers between devices: 9.85 us -> 38.5 us  [the longest x1 13.9 us: per_device(): lax.all_to_all(partial, ('blk', 'head'), 0, 0, tiled=True, axis_index_gro...]
    psum x1 -> x0, blocking collectives: 23.6 us -> none  [per_device(): squares = lax.psum(jnp.sum(mid_wide * mid_wide, axis=1), 'head')]
    dot_general x8 -> x1, matrix products: 19.2 us -> 0.27 us  [per_device(): jnp.dot(select, mid_state, preferred_element_type=jnp.float32)]
    pallas_call x0 -> x4, Pallas kernels: none -> 16.2 us  [the longest x1 5.53 us: hidden(): pl.pallas_call(functools.partial(hidden_kernel, steps), out_shape=jax.Sha...]
  transfers between devices with their start and end apart: 6 -> 9, of which waited for: 6 -> 8; matrix products, arithmetic and copies ran while one was open for 2% -> 3% of each run, Pallas kernels for 0% -> 2%
where the time goes in v1:
time: 265 us
  waiting for transfers between devices  156 us (59%)
  starting transfers between devices  42.8 us (16%)
  blocking collectives  21.8 us (8%)
  Pallas kernels  16.2 us (6%)
  between operations  13.3 us (5%)
  local copies, waits for them, and re-layouts  10.9 us (4%)
  other arithmetic  2.92 us (1%)
    all_gather x1, waiting for transfers between devices, per_device(): acts = lax.all_gather(act, 'head', axis=0, tiled=True)  41.7 us
    all_gather x1, waiting for transfers between devices, per_device(): lax.all_gather(incoming.reshape(SLOTS, 256), 'head', axis=0, tiled=True)  38.5 us
    all_to_all x1, waiting for transfers between devices, per_device(): lax.all_to_all(jnp.broadcast_to(half[None], (N_BLK,) + half.shape), 'blk'...  35.4 us
    all_to_all x1, blocking collectives, per_device(): lax.all_to_all(outgoing, 'blk', split_axis=0, concat_axis=0, tiled=True)  21.8 us
    all_to_all x1, waiting for transfers between devices, per_device(): lax.all_to_all(partial, ('blk', 'head'), 0, 0, tiled=True, axis_index_gro...  14.9 us
    all_to_all x1, waiting for transfers between devices, per_device(): lax.all_to_all(expert_out.reshape(EXPERTS, CAP, 256), 'blk', split_axis=0...  14.5 us
    all_to_all x1, starting transfers between devices, per_device(): lax.all_to_all(partial, ('blk', 'head'), 0, 0, tiled=True, axis_index_gro...  13.9 us
    all_to_all x1, starting transfers between devices, per_device(): lax.all_to_all(jnp.broadcast_to(half[None], (N_BLK,) + half.shape), 'blk'...  10.2 us
  transfers between devices with their start and end apart: 9, of which 8 were waited for; matrix products, arithmetic and copies ran while one was open for 3% of the time, Pallas kernels for 2%

profile of v1, /device:TPU:8, one launch (start us, length us, event | category | flops | bytes accessed | tf_op | source)
XLA Modules:
  0.0 264.6 jit_solution(5884007263423573876)
XLA Ops:
  7.4 1.2 broadcast_in_dim.12
  8.6 10.2 %all-to-all-start = ((bf16[32,32,576]{2,1,0:T(8,128)(2,1)}), bf16[32,32,576]{2,1,0:T(8,128)(2,1)S(1)}, u32[]{:S(2)}, u32[]{:S(2)}) async-start(bf16[32,32,576]{2,1,0:T(8,128)(2,1)} %broadcast_in_dim.12), calls=%async_computation | async-start | bytes 2621440 | tf_op jit(solution)/shard_map/all_to_all | solution.py:197
  19.5 35.4 %all-to-all-done = bf16[32,32,576]{2,1,0:T(8,128)(2,1)S(1)} async-done(((bf16[32,32,576]{2,1,0:T(8,128)(2,1)}), bf16[32,32,576]{2,1,0:T(8,128)(2,1)S(1)}, u32[]{:S(2)}, u32[]{:S(2)}) %all-to-all-start) | async-done | bytes 1179680 | tf_op jit(solution)/shard_map/all_to_all | solution.py:197
  55.0 1.5 copy.35
  56.5 1.9 collective-permute-start
  59.0 2.4 collective-permute-done
  61.4 1.4 copy.36.other_ref
  62.9 4.9 %attend.1 = bf16[64,512]{1,0:T(8,128)(2,1)} custom-call(s32[2]{0:T(128)} %pad_add_fusion.place_ref, bf16[64,2304]{1,0:T(8,128)(2,1)} %q_ref.1, bf16[1024,576]{1,0:T(8,128)(2,1)} %bitcast.40, bf16[1024,576]{1,0:T(8,128)(2,1)} %copy.36.other_ref, bf16[4,512,128]{2,1,0:T(8,128)(2,1)} %lift_ref.1), custom_call_target="tpu_custom_call" | custom-call | tf_op jit(solution)/shard_map/attend/pallas_call | solution.py:134
  67.7 1.6 broadcast_in_dim.13
  69.3 4.6 %all-to-all-start.1 = ((bf16[4,64,512]{2,1,0:T(8,128)(2,1)}), bf16[4,64,512]{2,1,0:T(8,128)(2,1)S(1)}, u32[]{:S(2)}, u32[]{:S(2)}) async-start(bf16[4,64,512]{2,1,0:T(8,128)(2,1)} %broadcast_in_dim.13), calls=%async_computation.1 | async-start | bytes 524288 | tf_op jit(solution)/shard_map/all_to_all | solution.py:209
  73.9 7.0 %all-to-all-done.1 = bf16[4,64,512]{2,1,0:T(8,128)(2,1)S(1)} async-done(((bf16[4,64,512]{2,1,0:T(8,128)(2,1)}), bf16[4,64,512]{2,1,0:T(8,128)(2,1)S(1)}, u32[]{:S(2)}, u32[]{:S(2)}) %all-to-all-start.1) | async-done | bytes 262176 | tf_op jit(solution)/shard_map/all_to_all | solution.py:209
  81.6 2.6 project.1
  84.1 13.9 %all-to-all-start.2 = ((bf16[64,32,128]{2,1,0:T(8,128)(2,1)}), bf16[64,32,128]{2,1,0:T(8,128)(2,1)S(1)}, u32[]{:S(2)}, u32[]{:S(2)}) async-start(bf16[64,32,128]{2,1,0:T(8,128)(2,1)} %project.1), calls=%async_computation.2 | async-start | bytes 1048576 | tf_op jit(solution)/shard_map/all_to_all | solution.py:218
  98.4 1.2 reduce-window.6
  100.2 14.9 %all-to-all-done.2 = bf16[64,32,128]{2,1,0:T(8,128)(2,1)S(1)} async-done(((bf16[64,32,128]{2,1,0:T(8,128)(2,1)}), bf16[64,32,128]{2,1,0:T(8,128)(2,1)S(1)}, u32[]{:S(2)}, u32[]{:S(2)}) %all-to-all-start.2) | async-done | bytes 524320 | tf_op jit(solution)/shard_map/all_to_all | solution.py:218
  115.2 2.2 collective-permute-start.1
  118.7 21.8 %all_to_all.25 = bf16[32,20,256]{2,1,0:T(8,128)(2,1)S(1)} all-to-all(bf16[32,20,256]{2,1,0:T(8,128)(2,1)S(1)} %reshape.86), channel_id=1, replica_groups=mesh['blk'=32,'head'=16] {'blk'}, dimensions={0} | all-to-all | bytes 655360 | tf_op jit(solution)/shard_map/all_to_all | solution.py:257
  141.3 38.5 %all-gather.6.cloned.1.call-done = bf16[10240,256]{1,0:T(8,128)(2,1)} async-done(((bf16[640,256]{1,0:T(8,128)(2,1)}), bf16[10240,256]{1,0:T(8,128)(2,1)}) %all-gather.6.cloned.1.call-update) | async-done | bytes 5242896 | tf_op jit(solution)/shard_map/all_gather | solution.py:258
  179.8 5.5 %hidden.1 = bf16[640,128]{1,0:T(8,128)(2,1)} custom-call(bf16[16,640,256]{2,1,0:T(8,128)(2,1)} %bitcast.41, bf16[4096,128]{1,0:T(8,128)(2,1)} %bitcast.43, bf16[4096,128]{1,0:T(8,128)(2,1)} %bitcast.44), custom_call_target="tpu_custom_call" | custom-call | tf_op jit(solution)/shard_map/hidden/pallas_call | solution.py:155
  185.4 41.7 %all-gather.8.cloned.1.call-done = bf16[10240,128]{1,0:T(8,128)(2,1)} async-done(((bf16[640,128]{1,0:T(8,128)(2,1)}), bf16[10240,128]{1,0:T(8,128)(2,1)}) %all-gather.8.cloned.1.call-update) | async-done | bytes 2621456 | tf_op jit(solution)/shard_map/all_gather | solution.py:260
  227.1 3.3 %down.1 = bf16[640,256]{1,0:T(8,128)(2,1)} custom-call(bf16[16,640,128]{2,1,0:T(8,128)(2,1)} %bitcast.42, bf16[2048,256]{1,0:T(8,128)(2,1)} %bitcast.47), custom_call_target="tpu_custom_call" | custom-call | tf_op jit(solution)/shard_map/down/pallas_call | solution.py:176
  230.3 1.8 reshape.90
  232.2 9.8 %all-to-all-start.4 = ((bf16[32,20,256]{2,1,0:T(8,128)(2,1)}), bf16[32,20,256]{2,1,0:T(8,128)(2,1)S(1)}, u32[]{:S(2)}, u32[]{:S(2)}) async-start(bf16[32,20,256]{2,1,0:T(8,128)(2,1)} %reshape.90), calls=%async_computation.4 | async-start | bytes 786432 | tf_op jit(solution)/shard_map/all_to_all | solution.py:262
  242.6 14.5 %all-to-all-done.4 = bf16[32,20,256]{2,1,0:T(8,128)(2,1)S(1)} async-done(((bf16[32,20,256]{2,1,0:T(8,128)(2,1)}), bf16[32,20,256]{2,1,0:T(8,128)(2,1)S(1)}, u32[]{:S(2)}, u32[]{:S(2)}) %all-to-all-start.4) | async-done | bytes 327712 | tf_op jit(solution)/shard_map/all_to_all | solution.py:262
  (46 shorter events, 7.6 us)
Async XLA Ops:
  6.5 0.9 copy-start
  8.6 46.4 %all-to-all-start = ((bf16[32,32,576]{2,1,0:T(8,128)(2,1)}), bf16[32,32,576]{2,1,0:T(8,128)(2,1)S(1)}, u32[]{:S(2)}, u32[]{:S(2)}) async-start(bf16[32,32,576]{2,1,0:T(8,128)(2,1)} %broadcast_in_dim.12), calls=%async_computation | async-start | bytes 2621440 | tf_op jit(solution)/shard_map/all_to_all | solution.py:197
  18.8 55.1 %all-gather.4.cloned.1.call-start = ((), (), s32[]{:S(2)}) async-start(), calls=%async_computation.5 | async-start | bytes 1179648 | tf_op jit(solution)/shard_map/all_gather | solution.py:202
  55.0 7.9 %copy-start.1 = (bf16[32,32,576]{2,1,0:T(8,128)(2,1)}, bf16[32,32,576]{2,1,0:T(8,128)(2,1)S(1)}, u32[]{:S(2)}) copy-start(bf16[32,32,576]{2,1,0:T(8,128)(2,1)S(1)} %all-to-all-done) | copy-start | bytes 3538948
  56.5 4.9 %collective-permute-start = (bf16[1024,576]{0,1:T(8,128)(2,1)}, bf16[1024,576]{0,1:T(8,128)(2,1)S(1)}, u32[]{:S(2)}, u32[]{:S(2)}) collective-permute-start(bf16[1024,576]{0,1:T(8,128)(2,1)} %copy.35), channel_id=1, source_target_pairs={{0,1},{1,0},{2,3},{3,2},{4,5},{5,4},{6,7},{7,6},{8,9},{9,8},{10,11... | collective-permute-start | bytes 3538952 | tf_op jit(solution)/shard_map/ppermute | solution.py:200
  69.3 11.6 %all-to-all-start.1 = ((bf16[4,64,512]{2,1,0:T(8,128)(2,1)}), bf16[4,64,512]{2,1,0:T(8,128)(2,1)S(1)}, u32[]{:S(2)}, u32[]{:S(2)}) async-start(bf16[4,64,512]{2,1,0:T(8,128)(2,1)} %broadcast_in_dim.13), calls=%async_computation.1 | async-start | bytes 524288 | tf_op jit(solution)/shard_map/all_to_all | solution.py:209
  80.8 0.7 copy-start.2
  81.5 16.5 %copy-start.4 = (s32[64,8]{0,1:T(8,128)S(1)}, s32[64,8]{0,1:T(8,128)}, u32[]{:S(2)}) copy-start(s32[64,8]{0,1:T(8,128)} %param.15) | copy-start | bytes 6148
  84.1 34.2 %copy-start.3 = (bf16[64,256]{1,0:T(8,128)(2,1)S(1)}, bf16[64,256]{1,0:T(8,128)(2,1)}, u32[]{:S(2)}) copy-start(bf16[64,256]{1,0:T(8,128)(2,1)} %param.10) | copy-start | bytes 98308
  84.1 31.0 %all-to-all-start.2 = ((bf16[64,32,128]{2,1,0:T(8,128)(2,1)}), bf16[64,32,128]{2,1,0:T(8,128)(2,1)S(1)}, u32[]{:S(2)}, u32[]{:S(2)}) async-start(bf16[64,32,128]{2,1,0:T(8,128)(2,1)} %project.1), calls=%async_computation.2 | async-start | bytes 1048576 | tf_op jit(solution)/shard_map/all_to_all | solution.py:218
  98.0 81.8 %all-gather.6.cloned.1.call-start = ((), (), s32[]{:S(2)}) async-start(), calls=%async_computation.6 | async-start | bytes 5570560 | tf_op jit(solution)/shard_map/all_gather | solution.py:258
  115.2 3.1 %collective-permute-start.1 = (f32[2,32,128]{2,1,0:T(8,128)S(1)}, f32[2,32,128]{2,1,0:T(8,128)S(1)}, u32[]{:S(2)}, u32[]{:S(2)}) collective-permute-start(f32[2,32,128]{2,1,0:T(8,128)S(1)} %constant_dynamic-slice_fusion), channel_id=1, source_target_pairs={{0,1},{1,0},{2,3},{3,2},{4,5},{5,4},{6,7},{7,6},{8,9},{9,8},{10,11... | collective-permute-start | bytes 98312 | tf_op jit(solution)/shard_map/ppermute | solution.py:224
  141.3 85.8 %all-gather.8.cloned.1.call-start = ((), (), s32[]{:S(2)}) async-start(), calls=%async_computation.7 | async-start | bytes 2785280 | tf_op jit(solution)/shard_map/all_gather | solution.py:260
  230.3 11.7 %copy-start.5 = (f32[64,8]{0,1:T(8,128)S(1)}, f32[64,8]{0,1:T(8,128)}, u32[]{:S(2)}) copy-start(f32[64,8]{0,1:T(8,128)} %param.16) | copy-start | bytes 6148
  232.2 24.9 %all-to-all-start.4 = ((bf16[32,20,256]{2,1,0:T(8,128)(2,1)}), bf16[32,20,256]{2,1,0:T(8,128)(2,1)S(1)}, u32[]{:S(2)}, u32[]{:S(2)}) async-start(bf16[32,20,256]{2,1,0:T(8,128)(2,1)} %reshape.90), calls=%async_computation.4 | async-start | bytes 786432 | tf_op jit(solution)/shard_map/all_to_all | solution.py:262
Sparse Core Ops, SparseCore 0:
  21.7 47.2 all-gather.3
  141.4 38.3 all-gather.5
  185.5 41.5 all-gather.7

commit v2 on v1

v2 whole, which is shorter than its diff:
```python
import functools

import jax
import jax.numpy as jnp
from jax import lax
from jax.experimental import pallas as pl
from jax.experimental.pallas import tpu as pltpu
from jax.sharding import PartitionSpec as P

D = 4096
LAT = 512
ROPE = 64
QKNOPE = 128
VDIM = 128
EXPERTS = 32
CAP = 20
SLOTS = EXPERTS * CAP
TOK = 64
HALF = TOK // 2
N_BLK = 32
N_HEAD = 16
N_X = 4
N_Y = 8
HEADS_HERE = 4
KEYS = N_BLK * HALF
SCALE = (QKNOPE + ROPE) ** (-0.5)

X_GROUPS = [[y * N_X + x for x in range(N_X)] for y in range(N_Y)]
Y_GROUPS = [[y * N_X + x for y in range(N_Y)] for x in range(N_X)]
XH_GROUPS = [[y * 64 + i for i in range(64)] for y in range(N_Y)]
QUAD = 4
PART = CAP // QUAD
ROWS = N_BLK * PART
QUADS = [[q * QUAD + i for i in range(QUAD)] for q in range(N_HEAD // QUAD)]
ACROSS = [[q * QUAD + i for q in range(N_HEAD // QUAD)] for i in range(QUAD)]
BLK_QUAD = [
    [b * N_HEAD + q * QUAD + i for b in range(N_BLK) for i in range(QUAD)]
    for q in range(N_HEAD // QUAD)
]
CORE_SWAP = [(i, i ^ 1) for i in range(N_HEAD)]
CHIP_SWAP = [(i, i ^ 2) for i in range(N_HEAD)]
Y_SWAPS = [[(b, b ^ (N_X * k)) for b in range(N_BLK)] for k in range(N_Y)]


def attention_kernel(place_ref, q_ref, own_ref, other_ref, lift_ref, out_ref):
    width = LAT + ROPE
    q_all = q_ref[...]
    q_rows = jnp.concatenate(
        [q_all[:, h * width : (h + 1) * width] for h in range(HEADS_HERE)], axis=0
    )
    rows = HEADS_HERE * TOK
    first = place_ref[0] * TOK
    core = place_ref[1]
    query_pos = first + (lax.broadcasted_iota(jnp.int32, (rows, N_Y * HALF), 0) & (TOK - 1))
    key_idx = lax.broadcasted_iota(jnp.int32, (rows, N_Y * HALF), 1)
    room = query_pos - ((key_idx >> 5) * (N_X * TOK) + (key_idx & (HALF - 1)))
    chunks = [
        (ref, x, x * TOK + part * HALF)
        for part, ref in ((core, own_ref), (1 - core, other_ref))
        for x in range(N_X)
    ]
    scores = []
    row_max = None
    for ref, x, offset in chunks:
        raw = jnp.dot(q_rows, ref[x], preferred_element_type=jnp.float32)
        raw = jnp.where(room >= offset, raw * SCALE, -1e30)
        scores.append(raw)
        row_max = raw if row_max is None else jnp.maximum(row_max, raw)
    row_max = jnp.max(row_max, axis=1, keepdims=True)
    total = 0.0
    context = 0.0
    for (ref, x, offset), raw in zip(chunks, scores):
        weights = jnp.where(room >= offset, jnp.exp(raw - row_max), 0.0)
        total = total + weights
        context = context + lax.dot_general(
            weights.astype(jnp.bfloat16),
            ref[x, :LAT],
            (((1,), (1,)), ((), ())),
            preferred_element_type=jnp.float32,
        )
    denominator = jnp.sum(total, axis=1, keepdims=True)
    context = (context / denominator).astype(jnp.bfloat16)
    for h in range(HEADS_HERE):
        lifted = jnp.dot(
            context[h * TOK : (h + 1) * TOK], lift_ref[h], preferred_element_type=jnp.float32
        ).astype(jnp.bfloat16)
        for x in range(N_X):
            out_ref[x, :, h * VDIM : (h + 1) * VDIM] = lifted


def project_kernel(place_ref, lifted_ref, *refs):
    proj_refs, out_ref = refs[:N_Y], refs[N_Y]
    lifted = lifted_ref[...]
    y = place_ref[0] // N_X
    for pair in range(N_Y // 2):
        weights = jnp.concatenate(
            [proj_refs[2 * pair][...], proj_refs[2 * pair + 1][...]], axis=1
        )
        full = jnp.dot(lifted, weights, preferred_element_type=jnp.float32).astype(jnp.bfloat16)
        for side in range(2):
            target = jnp.bitwise_xor(y, 2 * pair + side)
            for x in range(N_X):
                for p in range(2):
                    row = x * TOK + p * HALF
                    out_ref[x * 16 + target * 2 + p] = full[
                        row : row + HALF, side * 128 : (side + 1) * 128
                    ]


def hidden_kernel(place_ref, rows_ref, *refs):
    weight_refs, (out_ref, acc_ref, square_ref) = refs[:QUAD], refs[QUAD:]
    step = pl.program_id(0)

    @pl.when(step == 0)
    def _():
        acc_ref[...] = jnp.zeros_like(acc_ref)
        square_ref[...] = jnp.zeros_like(square_ref)

    rows = rows_ref[step]
    for j in range(QUAD):
        acc_ref[j] += jnp.dot(rows, weight_refs[j][...], preferred_element_type=jnp.float32)
    wide = rows.astype(jnp.float32)
    square_ref[...] += jnp.sum(wide * wide, axis=1, keepdims=True)

    @pl.when(step == QUAD - 1)
    def _():
        inverse = lax.rsqrt(square_ref[...] / D + 1e-06)
        for j in range(QUAD):
            owner = jnp.bitwise_xor(place_ref[2], j)
            gate = acc_ref[j, :, :128] * inverse
            up = acc_ref[j, :, 128:] * inverse
            act = (gate / (1.0 + jnp.exp(-gate)) * up).astype(jnp.bfloat16)
            for other in range(QUAD):

                @pl.when(owner == other)
                def _():
                    for q in range(QUAD):
                        out_ref[q, :, other * 128 : (other + 1) * 128] = act


def down_kernel(place_ref, act_ref, *refs):
    weight_refs, out_ref = refs[:QUAD], refs[QUAD]
    wide = jnp.concatenate([act_ref[i] for i in range(QUAD)], axis=1)
    for j in range(QUAD):
        owner = jnp.bitwise_xor(place_ref[2], j)
        result = jnp.dot(wide, weight_refs[j][...], preferred_element_type=jnp.float32).astype(
            jnp.bfloat16
        )
        for other in range(QUAD):

            @pl.when(owner == other)
            def _():
                out_ref[:, other * 256 : (other + 1) * 256] = result


def attend(place, queries, own, other, value_up):
    return pl.pallas_call(
        attention_kernel,
        out_shape=jax.ShapeDtypeStruct((N_X, TOK, HEADS_HERE * VDIM), jnp.bfloat16),
        in_specs=[pl.BlockSpec(memory_space=pltpu.SMEM)]
        + [pl.BlockSpec(memory_space=pltpu.VMEM)] * 4,
        out_specs=pl.BlockSpec(memory_space=pltpu.VMEM),
        name="attend",
    )(place, queries, own, other, value_up)


def project(place, lifted, proj):
    return pl.pallas_call(
        project_kernel,
        out_shape=jax.ShapeDtypeStruct((64, HALF, 128), jnp.bfloat16),
        in_specs=[pl.BlockSpec(memory_space=pltpu.SMEM)]
        + [pl.BlockSpec(memory_space=pltpu.VMEM)] * (1 + N_Y),
        out_specs=pl.BlockSpec(memory_space=pltpu.VMEM),
        name="project",
    )(place, lifted, *proj)


def hidden(place, rows, weights):
    depth = D // QUAD
    return pl.pallas_call(
        hidden_kernel,
        out_shape=jax.ShapeDtypeStruct((QUAD, ROWS, QUAD * 128), jnp.bfloat16),
        grid=(QUAD,),
        in_specs=[
            pl.BlockSpec(memory_space=pltpu.SMEM),
            pl.BlockSpec(memory_space=pltpu.VMEM),
        ]
        + [pl.BlockSpec((depth, 256), lambda i: (i, 0))] * QUAD,
        out_specs=pl.BlockSpec((QUAD, ROWS, QUAD * 128), lambda i: (0, 0, 0)),
        scratch_shapes=[
            pltpu.VMEM((QUAD, ROWS, 256), jnp.float32),
            pltpu.VMEM((ROWS, 1), jnp.float32),
        ],
        name="hidden",
    )(place, rows, *weights)


def down(place, act, weights):
    depth = QUAD * QUAD * 128
    return pl.pallas_call(
        down_kernel,
        out_shape=jax.ShapeDtypeStruct((ROWS, QUAD * 256), jnp.bfloat16),
        grid=(1,),
        in_specs=[
            pl.BlockSpec(memory_space=pltpu.SMEM),
            pl.BlockSpec(memory_space=pltpu.VMEM),
        ]
        + [pl.BlockSpec((depth, 256), lambda i: (D // depth, 0))] * QUAD,
        out_specs=pl.BlockSpec((ROWS, QUAD * 256), lambda i: (0, 0)),
        name="down",
    )(place, act, *weights)


def spread_over(x, axis, groups):
    count = len(groups[0])
    return lax.all_to_all(
        jnp.broadcast_to(x[None], (count,) + x.shape), axis, 0, 0, tiled=True, axis_index_groups=groups
    )


def per_device(
    tokens, queries, latents, value_up, out_proj, expert_ids, expert_gates, w_gate, w_up, w_down
):
    blk = lax.axis_index("blk")
    core = lax.axis_index("head") & 1

    weights = jnp.concatenate([jnp.concatenate([w_gate[0], w_up[0]], axis=1), w_down[0]], axis=0)
    weights_chip = lax.ppermute(weights, "head", CHIP_SWAP)
    weights_core = lax.ppermute(weights, "head", CORE_SWAP)
    weights_both = lax.ppermute(weights_chip, "head", CORE_SWAP)
    quad_weights = (weights, weights_core, weights_chip, weights_both)

    proj = [out_proj] + [lax.ppermute(out_proj, "blk", Y_SWAPS[j]) for j in range(1, N_Y)]

    half = lax.dynamic_slice(latents, (core * HALF, 0), (HALF, LAT + ROPE))
    column = spread_over(half, "blk", Y_GROUPS).reshape(N_Y * HALF, LAT + ROPE).T
    column, *proj[1:4] = lax.optimization_barrier((column, *proj[1:4]))
    own = spread_over(column, "blk", X_GROUPS).reshape(N_X, LAT + ROPE, N_Y * HALF)
    own, *proj[4:] = lax.optimization_barrier((own, *proj[4:]))
    other = lax.ppermute(own, "head", CORE_SWAP)

    place = jnp.stack([blk, core, lax.axis_index("head") & (QUAD - 1)]).astype(jnp.int32)
    lifted = attend(place, queries, own, other, value_up)

    lifted_row = lax.all_to_all(
        lifted, "blk", 0, 0, tiled=True, axis_index_groups=X_GROUPS
    ).reshape(N_X * TOK, lifted.shape[2])
    partial = project(place, lifted_row, proj)
    spread = lax.all_to_all(
        partial, ("blk", "head"), 0, 0, tiled=True, axis_index_groups=XH_GROUPS
    )
    summed = jnp.sum(spread.reshape(N_X, N_HEAD, HALF, 128).astype(jnp.float32), axis=1)
    keep = lax.dynamic_slice(summed, (2 * core, 0, 0), (2, HALF, 128))
    send = lax.dynamic_slice(summed, (2 - 2 * core, 0, 0), (2, HALF, 128))
    got = lax.ppermute(send, "head", CORE_SWAP)
    top = jnp.where(core == 0, keep, got)
    bottom = jnp.where(core == 0, got, keep)
    attended = jnp.concatenate([top, bottom], axis=1)
    attended = jnp.concatenate([attended[0], attended[1]], axis=1)
    mid_state = (tokens.astype(jnp.float32) + attended).astype(jnp.bfloat16)
    mid_wide = mid_state.astype(jnp.float32)

    row_count = tokens.shape[0]
    flat_ids = expert_ids.reshape(-1)
    choose_count = expert_ids.shape[1]
    onehot_ids = (flat_ids[:, None] == jnp.arange(EXPERTS, dtype=jnp.int32)[None, :]).astype(
        jnp.int32
    )
    earlier = jnp.cumsum(onehot_ids, axis=0) - onehot_ids
    ranks = jnp.sum(earlier * onehot_ids, axis=1)
    slot_ids = flat_ids * CAP + ranks
    slot_hits = jnp.arange(SLOTS, dtype=jnp.int32)[:, None] == slot_ids[None, :]
    select = jnp.sum(
        slot_hits.astype(jnp.bfloat16).reshape(SLOTS, row_count, choose_count), axis=2
    )
    combine = jnp.sum(
        jnp.where(slot_hits, expert_gates.reshape(-1)[None, :], 0.0).reshape(
            SLOTS, row_count, choose_count
        ),
        axis=2,
    )

    outgoing = (
        jnp.dot(select, mid_state, preferred_element_type=jnp.float32)
        .astype(jnp.bfloat16)
        .reshape(N_BLK * QUAD, PART * 2, 128)
    )
    incoming = lax.all_to_all(
        outgoing, ("blk", "head"), 0, 0, tiled=True, axis_index_groups=BLK_QUAD
    )
    rows_here = (
        incoming.reshape(N_BLK, QUAD, PART, 256).transpose(0, 2, 1, 3).reshape(ROWS, QUAD * 256)
    )
    rows = spread_over(rows_here, "head", ACROSS).reshape(QUAD, ROWS, QUAD * 256)
    act = hidden(place, rows, quad_weights)
    acts = lax.all_to_all(act, "head", 0, 0, tiled=True, axis_index_groups=ACROSS)
    expert_out = down(place, acts, quad_weights)
    sent = (
        expert_out.reshape(N_BLK, PART, QUAD, 256)
        .transpose(0, 2, 1, 3)
        .reshape(N_BLK * QUAD, PART * 2, 128)
    )
    returned = lax.all_to_all(
        sent, ("blk", "head"), 0, 0, tiled=True, axis_index_groups=BLK_QUAD
    )
    returned_wide = returned.reshape(SLOTS, 256).astype(jnp.float32)
    routed = jnp.einsum("sr,sd->rd", combine, returned_wide, precision=lax.Precision.HIGHEST)
    return (mid_wide + routed).astype(jnp.bfloat16)


def solution(mesh):
    placed = (
        P("blk", "head"),
        P("blk", "head"),
        P("blk", None),
        P("head", None, None),
        P("head", "blk"),
        P("blk", None),
        P("blk", None),
        P("blk", None, "head"),
        P("blk", None, "head"),
        P("blk", None, "head"),
    )
    return jax.shard_map(
        per_device, mesh=mesh, in_specs=placed, out_specs=P("blk", "head"), check_vma=False
    )
```

time: 265 us -> 275 us (1.038)
  waiting for transfers between devices: 156 us -> 92.5 us
  blocking collectives: 21.8 us -> 63.2 us
  starting transfers between devices: 42.8 us -> 75.1 us
  between operations: 13.3 us -> 0.43 us
  other arithmetic: 2.92 us -> 6.81 us
  Pallas kernels: 16.2 us -> 19.5 us
  local copies, waits for them, and re-layouts: 10.9 us -> 13.8 us
    all_gather x3 -> x0, waiting for transfers between devices: 80.2 us -> none  [the longest x1 41.7 us: per_device(): acts = lax.all_gather(act, 'head', axis=0, tiled=True)]
    all_to_all x1 -> x3, blocking collectives: 21.8 us -> 63.2 us  [the longest x1 28 us: per_device(): lax.all_to_all(outgoing, ('blk', 'head'), 0, 0, tiled=True, axis_index_gr...]
    ppermute x0 -> x10, starting transfers between devices: none -> 34.8 us  [the longest x7 26.9 us: per_device(): lax.ppermute(out_proj, 'blk', Y_SWAPS[j])]
    ppermute x0 -> x10, waiting for transfers between devices: none -> 19.2 us  [the longest x7 19.2 us: per_device(): lax.ppermute(out_proj, 'blk', Y_SWAPS[j])]
    all_to_all x3 -> x4, waiting for transfers between devices: 56.9 us -> 49.7 us  [the longest x3 30.6 us: spread_over(): lax.all_to_all(jnp.broadcast_to(x[None], (count,) + x.shape), axis, 0, 0,...]
    all_to_all x1, waiting for transfers between devices: 14.9 us -> 21 us  [per_device(): lax.all_to_all(partial, ('blk', 'head'), 0, 0, tiled=True, axis_index_gro...]
    pallas_call x3, Pallas kernels: 13.7 us -> 16.9 us  [the longest x1 6.7 us: hidden(): pl.pallas_call(hidden_kernel, out_shape=jax.ShapeDtypeStruct((QUAD, ROWS,...]
    all_to_all x3 -> x4, starting transfers between devices: 24.6 us -> 25.1 us  [the longest x3 17.7 us: spread_over(): lax.all_to_all(jnp.broadcast_to(x[None], (count,) + x.shape), axis, 0, 0,...]
  transfers between devices with their start and end apart: 9 -> 17, of which waited for: 8 -> 9; matrix products, arithmetic and copies ran while one was open for 3% -> 5% of each run, Pallas kernels for 2% -> 3%
where the time goes in v2:
time: 275 us; the launch traced here: 273 us
  waiting for transfers between devices  92.5 us (34%)
  starting transfers between devices  75.1 us (27%)
  blocking collectives  63.2 us (23%)
  Pallas kernels  19.5 us (7%)
  local copies, waits for them, and re-layouts  13.8 us (5%)
  other arithmetic  6.81 us (2%)
    all_to_all x3, waiting for transfers between devices, spread_over(): lax.all_to_all(jnp.broadcast_to(x[None], (count,) + x.shape), axis, 0, 0,...  30.6 us
    all_to_all x1, blocking collectives, per_device(): lax.all_to_all(outgoing, ('blk', 'head'), 0, 0, tiled=True, axis_index_gr...  28 us
    ppermute x7, starting transfers between devices, per_device(): lax.ppermute(out_proj, 'blk', Y_SWAPS[j])  26.9 us
    all_to_all x1, blocking collectives, per_device(): lax.all_to_all(act, 'head', 0, 0, tiled=True, axis_index_groups=ACROSS)  23.4 us
    all_to_all x1, waiting for transfers between devices, per_device(): lax.all_to_all(partial, ('blk', 'head'), 0, 0, tiled=True, axis_index_gro...  21 us
    ppermute x7, waiting for transfers between devices, per_device(): lax.ppermute(out_proj, 'blk', Y_SWAPS[j])  19.2 us
    all_to_all x1, waiting for transfers between devices, per_device(): lax.all_to_all(sent, ('blk', 'head'), 0, 0, tiled=True, axis_index_groups...  19.1 us
    all_to_all x3, starting transfers between devices, spread_over(): lax.all_to_all(jnp.broadcast_to(x[None], (count,) + x.shape), axis, 0, 0,...  17.7 us
  transfers between devices with their start and end apart: 17, of which 9 were waited for; matrix products, arithmetic and copies ran while one was open for 5% of the time, Pallas kernels for 3%

profile of v2, /device:TPU:8, one launch (start us, length us, event | category | flops | bytes accessed | tf_op | source)
XLA Modules:
  0.0 273.4 jit_solution(3772756850789409822)
XLA Ops:
  1.7 9.1 %all-to-all-start = ((bf16[8,32,576]{2,1,0:T(8,128)(2,1)}), bf16[8,32,576]{2,1,0:T(8,128)(2,1)S(1)}, u32[]{:S(2)}, u32[]{:S(2)}) async-start(bf16[8,32,576]{2,1,0:T(8,128)(2,1)} %broadcast_in_dim.20), calls=%async_computation | async-start | bytes 655360 | tf_op jit(solution)/shard_map/all_to_all | solution.py:216
  12.8 4.7 %collective-permute-start.1 = (bf16[512,128]{1,0:T(8,128)(2,1)}, bf16[512,128]{1,0:T(8,128)(2,1)S(1)}, u32[]{:S(2)}, u32[]{:S(2)}) collective-permute-start(bf16[512,128]{1,0:T(8,128)(2,1)} %refs_0_.1), channel_id=1, source_target_pairs={{0,128},{16,144},{32,160},{48,176},{64,192},{80,208},{96,224},{112... | collective-permute-start | bytes 393224 | tf_op jit(solution)/shard_map/ppermute | solution.py:233
  21.5 4.9 %collective-permute-done.1.refs_2_ = bf16[512,128]{1,0:T(8,128)(2,1)S(1)} collective-permute-done((bf16[512,128]{1,0:T(8,128)(2,1)}, bf16[512,128]{1,0:T(8,128)(2,1)S(1)}, u32[]{:S(2)}, u32[]{:S(2)}) %collective-permute-start.1) | collective-permute-done | bytes 131104 | tf_op jit(solution)/shard_map/ppermute | solution.py:233
  26.4 4.0 %collective-permute-done.2.refs_3_ = bf16[512,128]{1,0:T(8,128)(2,1)S(1)} collective-permute-done((bf16[512,128]{1,0:T(8,128)(2,1)}, bf16[512,128]{1,0:T(8,128)(2,1)S(1)}, u32[]{:S(2)}, u32[]{:S(2)}) %collective-permute-start.2) | collective-permute-done | bytes 131104 | tf_op jit(solution)/shard_map/ppermute | solution.py:233
  32.5 4.3 %all-to-all-start.1 = ((bf16[4,576,256]{2,1,0:T(8,128)(2,1)}), bf16[4,576,256]{2,1,0:T(8,128)(2,1)}, u32[]{:S(2)}, u32[]{:S(2)}) async-start(bf16[4,576,256]{2,1,0:T(8,128)(2,1)} %broadcast_in_dim.21), calls=%async_computation.1 | async-start | bytes 2359296 | tf_op jit(solution)/shard_map/all_to_all | solution.py:216
  39.0 3.7 %collective-permute-start.10 = (bf16[6144,256]{1,0:T(8,128)(2,1)S(1)}, bf16[6144,256]{1,0:T(8,128)(2,1)}, u32[]{:S(2)}, u32[]{:S(2)}) collective-permute-start(bf16[6144,256]{1,0:T(8,128)(2,1)S(1)} %pad_maximum_fusion.refs_0_), channel_id=1, source_target_pairs={{0,2},{1,3},{2,0},{3,1},{4,6},{5,7},{6,4},{7,5},{8,10},{9,11},{10,... | collective-permute-start | bytes 9437192 | tf_op jit(solution)/shard_map/ppermute | solution.py:228
  42.7 5.1 %collective-permute-start.3 = (bf16[512,128]{1,0:T(8,128)(2,1)S(1)}, bf16[512,128]{1,0:T(8,128)(2,1)S(1)}, u32[]{:S(2)}, u32[]{:S(2)}) collective-permute-start(bf16[512,128]{1,0:T(8,128)(2,1)S(1)} %copy-done.9), channel_id=1, source_target_pairs={{0,256},{16,272},{32,288},{48,304},{64,320},{80,336},{96,352},{112... | collective-permute-start | bytes 393224 | tf_op jit(solution)/shard_map/ppermute | solution.py:233
  47.7 2.8 %collective-permute-start.4 = (bf16[512,128]{1,0:T(8,128)(2,1)S(1)}, bf16[512,128]{1,0:T(8,128)(2,1)S(1)}, u32[]{:S(2)}, u32[]{:S(2)}) collective-permute-start(bf16[512,128]{1,0:T(8,128)(2,1)S(1)} %copy-done.9), channel_id=1, source_target_pairs={{0,320},{16,336},{32,352},{48,368},{64,256},{80,272},{96,288},{112... | collective-permute-start | bytes 393224 | tf_op jit(solution)/shard_map/ppermute | solution.py:233
  50.5 6.1 %collective-permute-start.5 = (bf16[512,128]{1,0:T(8,128)(2,1)S(1)}, bf16[512,128]{1,0:T(8,128)(2,1)S(1)}, u32[]{:S(2)}, u32[]{:S(2)}) collective-permute-start(bf16[512,128]{1,0:T(8,128)(2,1)S(1)} %copy-done.9), channel_id=1, source_target_pairs={{0,384},{16,400},{32,416},{48,432},{64,448},{80,464},{96,480},{112... | collective-permute-start | bytes 393224 | tf_op jit(solution)/shard_map/ppermute | solution.py:233
  56.6 3.8 %collective-permute-start.6 = (bf16[512,128]{1,0:T(8,128)(2,1)S(1)}, bf16[512,128]{1,0:T(8,128)(2,1)}, u32[]{:S(2)}, u32[]{:S(2)}) collective-permute-start(bf16[512,128]{1,0:T(8,128)(2,1)S(1)} %copy-done.9), channel_id=1, source_target_pairs={{0,448},{16,464},{32,480},{48,496},{64,384},{80,400},{96,416},{112... | collective-permute-start | bytes 393224 | tf_op jit(solution)/shard_map/ppermute | solution.py:233
  60.4 6.2 %collective-permute-done.4.refs_5_ = bf16[512,128]{1,0:T(8,128)(2,1)S(1)} collective-permute-done((bf16[512,128]{1,0:T(8,128)(2,1)S(1)}, bf16[512,128]{1,0:T(8,128)(2,1)S(1)}, u32[]{:S(2)}, u32[]{:S(2)}) %collective-permute-start.4) | collective-permute-done | bytes 131104 | tf_op jit(solution)/shard_map/ppermute | solution.py:233
  74.9 4.9 %attend.1 = bf16[4,64,512]{2,1,0:T(8,128)(2,1)} custom-call(s32[3]{0:T(128)} %pad_add_fusion.place_ref, bf16[64,2304]{1,0:T(8,128)(2,1)} %q_ref.1, bf16[4,576,256]{2,1,0:T(8,128)(2,1)} %all-to-all-done.1.own_ref, bf16[4,576,256]{2,1,0:T(8,128)(2,1)} %collective-permute-done.7.other_ref, bf16[4,512,128]{2,1,0:T(8,128)(2,1)} %lift_ref.1), custom_call_target="tpu_custom_call" | custom-call | tf_op jit(solution)/shard_map/attend/pallas_call | solution.py:157
  79.8 11.8 %all_to_all.40 = bf16[4,64,512]{2,1,0:T(8,128)(2,1)} all-to-all(bf16[4,64,512]{2,1,0:T(8,128)(2,1)} %attend.1), channel_id=1, replica_groups={{0,16,32,48},{64,80,96,112},{128,144,160,176},{192,208,224,240},{256,27..., dimensions={0} | all-to-all | bytes 524288 | tf_op jit(solution)/shard_map/all_to_all | solution.py:245
  91.6 2.6 project.1
  94.3 11.3 %all-to-all-start.3 = ((bf16[64,32,128]{2,1,0:T(8,128)(2,1)}), bf16[64,32,128]{2,1,0:T(8,128)(2,1)}, u32[]{:S(2)}, u32[]{:S(2)}) async-start(bf16[64,32,128]{2,1,0:T(8,128)(2,1)} %project.1), calls=%async_computation.3 | async-start | bytes 1048576 | tf_op jit(solution)/shard_map/all_to_all | solution.py:249
  109.6 21.0 %all-to-all-done.3 = bf16[64,32,128]{2,1,0:T(8,128)(2,1)} async-done(((bf16[64,32,128]{2,1,0:T(8,128)(2,1)}), bf16[64,32,128]{2,1,0:T(8,128)(2,1)}, u32[]{:S(2)}, u32[]{:S(2)}) %all-to-all-start.3) | async-done | bytes 524320 | tf_op jit(solution)/shard_map/all_to_all | solution.py:249
  140.0 28.0 %all_to_all.41 = bf16[128,10,128]{2,1,0:T(8,128)(2,1)} all-to-all(bf16[128,10,128]{2,1,0:T(8,128)(2,1)} %reshape.80), channel_id=1, replica_groups={{0,1,2,3,16,17,18,19,32,33,34,35,48,49,50,51,64,65,66,67,80,81,82,83,96..., dimensions={0} | all-to-all | bytes 655360 | tf_op jit(solution)/shard_map/all_to_all | solution.py:288
  172.4 4.3 %all-to-all-start.5 = ((bf16[4,160,1024]{2,1,0:T(8,128)(2,1)}), bf16[4,160,1024]{2,1,0:T(8,128)(2,1)}, u32[]{:S(2)}, u32[]{:S(2)}) async-start(bf16[4,160,1024]{2,1,0:T(8,128)(2,1)} %broadcast_in_dim.39), calls=%async_computation.5 | async-start | bytes 2621440 | tf_op jit(solution)/shard_map/all_to_all | solution.py:216
  176.8 30.6 %all-to-all-done.5.rows_ref = bf16[4,160,1024]{2,1,0:T(8,128)(2,1)} async-done(((bf16[4,160,1024]{2,1,0:T(8,128)(2,1)}), bf16[4,160,1024]{2,1,0:T(8,128)(2,1)}, u32[]{:S(2)}, u32[]{:S(2)}) %all-to-all-start.5) | async-done | bytes 1310752 | tf_op jit(solution)/shard_map/all_to_all | solution.py:216
  207.4 6.7 %hidden.1 = bf16[4,160,512]{2,1,0:T(8,128)(2,1)} custom-call(s32[3]{0:T(128)} %pad_add_fusion.place_ref, bf16[4,160,1024]{2,1,0:T(8,128)(2,1)} %all-to-all-done.5.rows_ref, bf16[6144,256]{1,0:T(8,128)(2,1)} %copy-done.1, bf16[6144,256]{1,0:T(8,128)(2,1)} %collective-permute-done.9.refs_1_, bf16[6144,256]{1,0:T(8,128)(2,1)} %collective-permute-done.10.refs_2_, ...), custom_call_target="tpu_custom_call" | custom-call | tf_op jit(solution)/shard_map/hidden/pallas_call | solution.py:180
  214.1 23.4 %all_to_all.42.act_ref = bf16[4,160,512]{2,1,0:T(8,128)(2,1)} all-to-all(bf16[4,160,512]{2,1,0:T(8,128)(2,1)} %hidden.1), channel_id=1, replica_groups={{0,4,8,12},{1,5,9,13},{2,6,10,14},{3,7,11,15},{16,20,24,28},{17,21,25,2..., dimensions={0} | all-to-all | bytes 1310720 | tf_op jit(solution)/shard_map/all_to_all | solution.py:296
  237.5 5.3 %down.1 = bf16[160,1024]{1,0:T(8,128)(2,1)} custom-call(s32[3]{0:T(128)} %pad_add_fusion.place_ref, bf16[4,160,512]{2,1,0:T(8,128)(2,1)} %all_to_all.42.act_ref, bf16[6144,256]{1,0:T(8,128)(2,1)} %copy-done.1, bf16[6144,256]{1,0:T(8,128)(2,1)} %collective-permute-done.9.refs_1_, bf16[6144,256]{1,0:T(8,128)(2,1)} %collective-permute-done.10.refs_2_, ...), custom_call_target="tpu_custom_call" | custom-call | tf_op jit(solution)/shard_map/down/pallas_call | solution.py:200
  245.2 7.4 %all-to-all-start.7 = ((bf16[128,10,128]{2,1,0:T(8,128)(2,1)}), bf16[128,10,128]{2,1,0:T(8,128)(2,1)S(1)}, u32[]{:S(2)}, u32[]{:S(2)}) async-start(bf16[128,10,128]{2,1,0:T(8,128)(2,1)} %reshape.83), calls=%async_computation.7 | async-start | bytes 1048576 | tf_op jit(solution)/shard_map/all_to_all | solution.py:303
  253.1 19.1 %all-to-all-done.7 = bf16[128,10,128]{2,1,0:T(8,128)(2,1)S(1)} async-done(((bf16[128,10,128]{2,1,0:T(8,128)(2,1)}), bf16[128,10,128]{2,1,0:T(8,128)(2,1)S(1)}, u32[]{:S(2)}, u32[]{:S(2)}) %all-to-all-start.7) | async-done | bytes 327712 | tf_op jit(solution)/shard_map/all_to_all | solution.py:303
  (90 shorter events, 41.9 us)
Async XLA Ops:
  1.7 28.8 %all-to-all-start = ((bf16[8,32,576]{2,1,0:T(8,128)(2,1)}), bf16[8,32,576]{2,1,0:T(8,128)(2,1)S(1)}, u32[]{:S(2)}, u32[]{:S(2)}) async-start(bf16[8,32,576]{2,1,0:T(8,128)(2,1)} %broadcast_in_dim.20), calls=%async_computation | async-start | bytes 655360 | tf_op jit(solution)/shard_map/all_to_all | solution.py:216
  10.8 10.7 %collective-permute-start = (bf16[512,128]{1,0:T(8,128)(2,1)}, bf16[512,128]{1,0:T(8,128)(2,1)S(1)}, u32[]{:S(2)}, u32[]{:S(2)}) collective-permute-start(bf16[512,128]{1,0:T(8,128)(2,1)} %refs_0_.1), channel_id=1, source_target_pairs={{0,64},{16,80},{32,96},{48,112},{64,0},{80,16},{96,32},{112,48},{1... | collective-permute-start | bytes 393224 | tf_op jit(solution)/shard_map/ppermute | solution.py:233
  12.8 13.6 %collective-permute-start.1 = (bf16[512,128]{1,0:T(8,128)(2,1)}, bf16[512,128]{1,0:T(8,128)(2,1)S(1)}, u32[]{:S(2)}, u32[]{:S(2)}) collective-permute-start(bf16[512,128]{1,0:T(8,128)(2,1)} %refs_0_.1), channel_id=1, source_target_pairs={{0,128},{16,144},{32,160},{48,176},{64,192},{80,208},{96,224},{112... | collective-permute-start | bytes 393224 | tf_op jit(solution)/shard_map/ppermute | solution.py:233
  17.5 12.9 %collective-permute-start.2 = (bf16[512,128]{1,0:T(8,128)(2,1)}, bf16[512,128]{1,0:T(8,128)(2,1)S(1)}, u32[]{:S(2)}, u32[]{:S(2)}) collective-permute-start(bf16[512,128]{1,0:T(8,128)(2,1)} %refs_0_.1), channel_id=1, source_target_pairs={{0,192},{16,208},{32,224},{48,240},{64,128},{80,144},{96,160},{112... | collective-permute-start | bytes 393224 | tf_op jit(solution)/shard_map/ppermute | solution.py:233
  32.5 37.4 %all-to-all-start.1 = ((bf16[4,576,256]{2,1,0:T(8,128)(2,1)}), bf16[4,576,256]{2,1,0:T(8,128)(2,1)}, u32[]{:S(2)}, u32[]{:S(2)}) async-start(bf16[4,576,256]{2,1,0:T(8,128)(2,1)} %broadcast_in_dim.21), calls=%async_computation.1 | async-start | bytes 2359296 | tf_op jit(solution)/shard_map/all_to_all | solution.py:216
  39.0 66.6 %copy-start.1 = (bf16[6144,256]{1,0:T(8,128)(2,1)}, bf16[6144,256]{1,0:T(8,128)(2,1)S(1)}, u32[]{:S(2)}) copy-start(bf16[6144,256]{1,0:T(8,128)(2,1)S(1)} %pad_maximum_fusion.refs_0_) | copy-start | bytes 9437188
  39.0 95.9 %collective-permute-start.10 = (bf16[6144,256]{1,0:T(8,128)(2,1)S(1)}, bf16[6144,256]{1,0:T(8,128)(2,1)}, u32[]{:S(2)}, u32[]{:S(2)}) collective-permute-start(bf16[6144,256]{1,0:T(8,128)(2,1)S(1)} %pad_maximum_fusion.refs_0_), channel_id=1, source_target_pairs={{0,2},{1,3},{2,0},{3,1},{4,6},{5,7},{6,4},{7,5},{8,10},{9,11},{10,... | collective-permute-start | bytes 9437192 | tf_op jit(solution)/shard_map/ppermute | solution.py:228
  42.7 17.7 %collective-permute-start.3 = (bf16[512,128]{1,0:T(8,128)(2,1)S(1)}, bf16[512,128]{1,0:T(8,128)(2,1)S(1)}, u32[]{:S(2)}, u32[]{:S(2)}) collective-permute-start(bf16[512,128]{1,0:T(8,128)(2,1)S(1)} %copy-done.9), channel_id=1, source_target_pairs={{0,256},{16,272},{32,288},{48,304},{64,320},{80,336},{96,352},{112... | collective-permute-start | bytes 393224 | tf_op jit(solution)/shard_map/ppermute | solution.py:233
  47.7 18.9 %collective-permute-start.4 = (bf16[512,128]{1,0:T(8,128)(2,1)S(1)}, bf16[512,128]{1,0:T(8,128)(2,1)S(1)}, u32[]{:S(2)}, u32[]{:S(2)}) collective-permute-start(bf16[512,128]{1,0:T(8,128)(2,1)S(1)} %copy-done.9), channel_id=1, source_target_pairs={{0,320},{16,336},{32,352},{48,368},{64,256},{80,272},{96,288},{112... | collective-permute-start | bytes 393224 | tf_op jit(solution)/shard_map/ppermute | solution.py:233
  50.5 18.7 %collective-permute-start.5 = (bf16[512,128]{1,0:T(8,128)(2,1)S(1)}, bf16[512,128]{1,0:T(8,128)(2,1)S(1)}, u32[]{:S(2)}, u32[]{:S(2)}) collective-permute-start(bf16[512,128]{1,0:T(8,128)(2,1)S(1)} %copy-done.9), channel_id=1, source_target_pairs={{0,384},{16,400},{32,416},{48,432},{64,448},{80,464},{96,480},{112... | collective-permute-start | bytes 393224 | tf_op jit(solution)/shard_map/ppermute | solution.py:233
  56.6 13.3 %collective-permute-start.6 = (bf16[512,128]{1,0:T(8,128)(2,1)S(1)}, bf16[512,128]{1,0:T(8,128)(2,1)}, u32[]{:S(2)}, u32[]{:S(2)}) collective-permute-start(bf16[512,128]{1,0:T(8,128)(2,1)S(1)} %copy-done.9), channel_id=1, source_target_pairs={{0,448},{16,464},{32,480},{48,496},{64,384},{80,400},{96,416},{112... | collective-permute-start | bytes 393224 | tf_op jit(solution)/shard_map/ppermute | solution.py:233
  60.4 31.2 %copy-start.13 = (bf16[512,128]{1,0:T(8,128)(2,1)}, bf16[512,128]{1,0:T(8,128)(2,1)S(1)}, u32[]{:S(2)}) copy-start(bf16[512,128]{1,0:T(8,128)(2,1)S(1)} %collective-permute-done.3.refs_4_) | copy-start | bytes 393220
  69.8 5.1 %collective-permute-start.7 = (bf16[4,576,256]{2,1,0:T(8,128)(2,1)}, bf16[4,576,256]{2,1,0:T(8,128)(2,1)}, u32[]{:S(2)}, u32[]{:S(2)}) collective-permute-start(bf16[4,576,256]{2,1,0:T(8,128)(2,1)} %all-to-all-done.1.own_ref), channel_id=1, source_target_pairs={{0,1},{1,0},{2,3},{3,2},{4,5},{5,4},{6,7},{7,6},{8,9},{9,8},{10,11... | collective-permute-start | bytes 3538952 | tf_op jit(solution)/shard_map/ppermute | solution.py:240
  72.3 35.1 %copy-start.16 = (s32[64,8]{0,1:T(8,128)S(1)}, s32[64,8]{0,1:T(8,128)}, u32[]{:S(2)}) copy-start(s32[64,8]{0,1:T(8,128)} %param.15) | copy-start | bytes 6148
  94.3 36.3 %all-to-all-start.3 = ((bf16[64,32,128]{2,1,0:T(8,128)(2,1)}), bf16[64,32,128]{2,1,0:T(8,128)(2,1)}, u32[]{:S(2)}, u32[]{:S(2)}) async-start(bf16[64,32,128]{2,1,0:T(8,128)(2,1)} %project.1), calls=%async_computation.3 | async-start | bytes 1048576 | tf_op jit(solution)/shard_map/all_to_all | solution.py:249
  105.6 71.2 %collective-permute-start.9 = (bf16[6144,256]{1,0:T(8,128)(2,1)S(1)}, bf16[6144,256]{1,0:T(8,128)(2,1)}, u32[]{:S(2)}, u32[]{:S(2)}) collective-permute-start(bf16[6144,256]{1,0:T(8,128)(2,1)S(1)} %pad_maximum_fusion.refs_0_), channel_id=1, source_target_pairs={{0,1},{1,0},{2,3},{3,2},{4,5},{5,4},{6,7},{7,6},{8,9},{9,8},{10,11... | collective-permute-start | bytes 9437192 | tf_op jit(solution)/shard_map/ppermute | solution.py:229
  109.6 27.6 %copy-start.2 = (s32[64,8]{1,0:T(8,128)}, s32[64,8]{1,0:T(8,128)S(1)}, u32[]{:S(2)}) copy-start(s32[64,8]{1,0:T(8,128)S(1)} %copy.46) | copy-start | bytes 6148
  131.7 5.4 %collective-permute-start.8 = (f32[2,32,128]{2,1,0:T(8,128)S(1)}, f32[2,32,128]{2,1,0:T(8,128)S(1)}, u32[]{:S(2)}, u32[]{:S(2)}) collective-permute-start(f32[2,32,128]{2,1,0:T(8,128)S(1)} %constant_dynamic-slice_fusion), channel_id=1, source_target_pairs={{0,1},{1,0},{2,3},{3,2},{4,5},{5,4},{6,7},{7,6},{8,9},{9,8},{10,11... | collective-permute-start | bytes 98312 | tf_op jit(solution)/shard_map/ppermute | solution.py:255
  134.8 42.0 %collective-permute-start.11 = (bf16[6144,256]{1,0:T(8,128)(2,1)}, bf16[6144,256]{1,0:T(8,128)(2,1)}, u32[]{:S(2)}, u32[]{:S(2)}) collective-permute-start(bf16[6144,256]{1,0:T(8,128)(2,1)} %collective-permute-done.10.refs_2_), channel_id=1, source_target_pairs={{0,1},{1,0},{2,3},{3,2},{4,5},{5,4},{6,7},{7,6},{8,9},{9,8},{10,11... | collective-permute-start | bytes 9437192 | tf_op jit(solution)/shard_map/ppermute | solution.py:230
  172.4 35.0 %all-to-all-start.5 = ((bf16[4,160,1024]{2,1,0:T(8,128)(2,1)}), bf16[4,160,1024]{2,1,0:T(8,128)(2,1)}, u32[]{:S(2)}, u32[]{:S(2)}) async-start(bf16[4,160,1024]{2,1,0:T(8,128)(2,1)} %broadcast_in_dim.39), calls=%async_computation.5 | async-start | bytes 2621440 | tf_op jit(solution)/shard_map/all_to_all | solution.py:216
  242.8 29.6 %copy-start.5 = (f32[64,128]{1,0:T(8,128)S(1)}, f32[64,128]{1,0:T(8,128)}, u32[]{:S(2)}) copy-start(f32[64,128]{1,0:T(8,128)} %copy-done.4) | copy-start | bytes 98308
  242.8 29.7 %copy-start.7 = (f32[64,128]{1,0:T(8,128)S(1)}, f32[64,128]{1,0:T(8,128)}, u32[]{:S(2)}) copy-start(f32[64,128]{1,0:T(8,128)} %copy-done.6) | copy-start | bytes 98308
  242.8 29.7 %copy-start.8 = (bf16[64,256]{1,0:T(8,128)(2,1)S(1)}, bf16[64,256]{1,0:T(8,128)(2,1)}, u32[]{:S(2)}) copy-start(bf16[64,256]{1,0:T(8,128)(2,1)} %param.10) | copy-start | bytes 98308
  245.2 27.1 %all-to-all-start.7 = ((bf16[128,10,128]{2,1,0:T(8,128)(2,1)}), bf16[128,10,128]{2,1,0:T(8,128)(2,1)S(1)}, u32[]{:S(2)}, u32[]{:S(2)}) async-start(bf16[128,10,128]{2,1,0:T(8,128)(2,1)} %reshape.83), calls=%async_computation.7 | async-start | bytes 1048576 | tf_op jit(solution)/shard_map/all_to_all | solution.py:303
  (11 other events, 53.0 us)

commit v3 on v2

--- a/solution.py
+++ b/solution.py
@@ -1,11 +1,10 @@
-import functools
-
 import jax
 import jax.numpy as jnp
 from jax import lax
 from jax.experimental import pallas as pl
 from jax.experimental.pallas import tpu as pltpu
 from jax.sharding import PartitionSpec as P
+
 
 D = 4096
 LAT = 512
@@ -22,12 +21,34 @@
 N_X = 4
 N_Y = 8
 HEADS_HERE = 4
-KEYS = N_BLK * HALF
 SCALE = (QKNOPE + ROPE) ** (-0.5)
 
 X_GROUPS = [[y * N_X + x for x in range(N_X)] for y in range(N_Y)]
 Y_GROUPS = [[y * N_X + x for y in range(N_Y)] for x in range(N_X)]
-XH_GROUPS = [[y * 64 + i for i in range(64)] for y in range(N_Y)]
+N_Z = N_HEAD // 2
+
+
+def device(y, x, z, core):
+    return (y * N_X + x) * N_HEAD + z * 2 + core
+
+
+XC_GROUPS = [
+    [device(y, x, z, c) for x in range(N_X) for c in range(2)]
+    for y in range(N_Y)
+    for z in range(N_Z)
+]
+XZ_GROUPS = [
+    [device(y, x, z, c) for x in range(N_X) for z in range(N_Z)]
+    for y in range(N_Y)
+    for c in range(2)
+]
+PROJ_MOVE = [
+    (device(y, x, z, c), device((y & 6) | c, x, z, y & 1))
+    for y in range(N_Y)
+    for x in range(N_X)
+    for z in range(N_Z)
+    for c in range(2)
+]
 QUAD = 4
 PART = CAP // QUAD
 ROWS = N_BLK * PART
@@ -39,7 +60,7 @@
 ]
 CORE_SWAP = [(i, i ^ 1) for i in range(N_HEAD)]
 CHIP_SWAP = [(i, i ^ 2) for i in range(N_HEAD)]
-Y_SWAPS = [[(b, b ^ (N_X * k)) for b in range(N_BLK)] for k in range(N_Y)]
+BOTH_SWAP = [(i, i ^ 3) for i in range(N_HEAD)]
 
 
 def attention_kernel(place_ref, q_ref, own_ref, other_ref, lift_ref, out_ref):
@@ -84,27 +105,49 @@
         lifted = jnp.dot(
             context[h * TOK : (h + 1) * TOK], lift_ref[h], preferred_element_type=jnp.float32
         ).astype(jnp.bfloat16)
-        for x in range(N_X):
-            out_ref[x, :, h * VDIM : (h + 1) * VDIM] = lifted
-
-
-def project_kernel(place_ref, lifted_ref, *refs):
-    proj_refs, out_ref = refs[:N_Y], refs[N_Y]
-    lifted = lifted_ref[...]
-    y = place_ref[0] // N_X
-    for pair in range(N_Y // 2):
-        weights = jnp.concatenate(
-            [proj_refs[2 * pair][...], proj_refs[2 * pair + 1][...]], axis=1
-        )
+        for member in range(2 * N_X):
+            out_ref[member, :, h * VDIM : (h + 1) * VDIM] = lifted
+
+
+def project_kernel(lifted_ref, proj_ref, out_ref):
+    halves = [
+        jnp.concatenate([lifted_ref[x * 2 + c] for x in range(N_X)], axis=0) for c in range(2)
+    ]
+    lifted = jnp.concatenate(halves, axis=1)
+    for pair in range(N_Y // 4):
+        weights = jnp.concatenate([proj_ref[2 * pair], proj_ref[2 * pair + 1]], axis=1)
         full = jnp.dot(lifted, weights, preferred_element_type=jnp.float32).astype(jnp.bfloat16)
         for side in range(2):
-            target = jnp.bitwise_xor(y, 2 * pair + side)
             for x in range(N_X):
                 for p in range(2):
                     row = x * TOK + p * HALF
-                    out_ref[x * 16 + target * 2 + p] = full[
+                    out_ref[x * N_Z + (2 * pair + side) * 2 + p] = full[
                         row : row + HALF, side * 128 : (side + 1) * 128
                     ]
+
+
+def mid_kernel(place_ref, attended_ref, *refs):
+    token_refs, (quad_ref, own_ref) = refs[:QUAD], refs[QUAD:]
+    me = place_ref[2]
+    for j in range(QUAD):
+        owner = jnp.bitwise_xor(me, j)
+        core = owner // 2
+        first = (owner % 2) * 2
+        for p in range(2):
+            rows = slice(p * HALF, (p + 1) * HALF)
+            wide = [
+                token_refs[j][rows, i * 128 : (i + 1) * 128].astype(jnp.float32)
+                + attended_ref[p * 2 + core, first + i]
+                for i in range(2)
+            ]
+            mid = jnp.concatenate(wide, axis=1).astype(jnp.bfloat16)
+            if j == 0:
+                own_ref[rows, :] = mid
+            for other in range(QUAD):
+
+                @pl.when(owner == other)
+                def _():
+                    quad_ref[rows, other * 256 : (other + 1) * 256] = mid
 
 
 def hidden_kernel(place_ref, rows_ref, *refs):
@@ -156,7 +199,7 @@
 def attend(place, queries, own, other, value_up):
     return pl.pallas_call(
         attention_kernel,
-        out_shape=jax.ShapeDtypeStruct((N_X, TOK, HEADS_HERE * VDIM), jnp.bfloat16),
+        out_shape=jax.ShapeDtypeStruct((2 * N_X, TOK, HEADS_HERE * VDIM), jnp.bfloat16),
         in_specs=[pl.BlockSpec(memory_space=pltpu.SMEM)]
         + [pl.BlockSpec(memory_space=pltpu.VMEM)] * 4,
         out_specs=pl.BlockSpec(memory_space=pltpu.VMEM),
@@ -164,15 +207,28 @@
     )(place, queries, own, other, value_up)
 
 
-def project(place, lifted, proj):
+def project(lifted, proj):
     return pl.pallas_call(
         project_kernel,
-        out_shape=jax.ShapeDtypeStruct((64, HALF, 128), jnp.bfloat16),
-        in_specs=[pl.BlockSpec(memory_space=pltpu.SMEM)]
-        + [pl.BlockSpec(memory_space=pltpu.VMEM)] * (1 + N_Y),
+        out_shape=jax.ShapeDtypeStruct((N_X * N_Z, HALF, 128), jnp.bfloat16),
+        in_specs=[pl.BlockSpec(memory_space=pltpu.VMEM)] * 2,
         out_specs=pl.BlockSpec(memory_space=pltpu.VMEM),
         name="project",
-    )(place, lifted, *proj)
+    )(lifted, proj)
+
+
+def middle(place, attended, tokens):
+    return pl.pallas_call(
+        mid_kernel,
+        out_shape=(
+            jax.ShapeDtypeStruct((TOK, QUAD * 256), jnp.bfloat16),
+            jax.ShapeDtypeStruct((TOK, 256), jnp.bfloat16),
+        ),
+        in_specs=[pl.BlockSpec(memory_space=pltpu.SMEM)]
+        + [pl.BlockSpec(memory_space=pltpu.VMEM)] * (1 + QUAD),
+        out_specs=(pl.BlockSpec(memory_space=pltpu.VMEM),) * 2,
+        name="middle",
+    )(place, attended, *tokens)
 
 
 def hidden(place, rows, weights):
@@ -196,17 +252,12 @@
 
 
 def down(place, act, weights):
-    depth = QUAD * QUAD * 128
     return pl.pallas_call(
         down_kernel,
         out_shape=jax.ShapeDtypeStruct((ROWS, QUAD * 256), jnp.bfloat16),
-        grid=(1,),
-        in_specs=[
-            pl.BlockSpec(memory_space=pltpu.SMEM),
-            pl.BlockSpec(memory_space=pltpu.VMEM),
-        ]
-        + [pl.BlockSpec((depth, 256), lambda i: (D // depth, 0))] * QUAD,
-        out_specs=pl.BlockSpec((ROWS, QUAD * 256), lambda i: (0, 0)),
+        in_specs=[pl.BlockSpec(memory_space=pltpu.SMEM)]
+        + [pl.BlockSpec(memory_space=pltpu.VMEM)] * (1 + QUAD),
+        out_specs=pl.BlockSpec(memory_space=pltpu.VMEM),
         name="down",
     )(place, act, *weights)
 
@@ -216,6 +267,11 @@
     return lax.all_to_all(
         jnp.broadcast_to(x[None], (count,) + x.shape), axis, 0, 0, tiled=True, axis_index_groups=groups
     )
+
+
+def quad_of(own, chip):
+    core = lax.ppermute(own, "head", CORE_SWAP)
+    return (own, core, chip, lax.ppermute(chip, "head", CORE_SWAP))
 
 
 def per_device(
@@ -224,40 +280,37 @@
     blk = lax.axis_index("blk")
     core = lax.axis_index("head") & 1
 
-    weights = jnp.concatenate([jnp.concatenate([w_gate[0], w_up[0]], axis=1), w_down[0]], axis=0)
-    weights_chip = lax.ppermute(weights, "head", CHIP_SWAP)
-    weights_core = lax.ppermute(weights, "head", CORE_SWAP)
-    weights_both = lax.ppermute(weights_chip, "head", CORE_SWAP)
-    quad_weights = (weights, weights_core, weights_chip, weights_both)
-
-    proj = [out_proj] + [lax.ppermute(out_proj, "blk", Y_SWAPS[j]) for j in range(1, N_Y)]
+    quad_tokens = [tokens] + [
+        lax.ppermute(tokens, "head", swap) for swap in (CORE_SWAP, CHIP_SWAP, BOTH_SWAP)
+    ]
+    moved = lax.ppermute(out_proj, ("blk", "head"), PROJ_MOVE)
+    proj = lax.all_gather(moved, "blk", axis=0, tiled=True, axis_index_groups=Y_GROUPS)
+    proj = proj.reshape(N_Y // 2, 2 * out_proj.shape[0], 128)
 
     half = lax.dynamic_slice(latents, (core * HALF, 0), (HALF, LAT + ROPE))
     column = spread_over(half, "blk", Y_GROUPS).reshape(N_Y * HALF, LAT + ROPE).T
-    column, *proj[1:4] = lax.optimization_barrier((column, *proj[1:4]))
+    column, *quad_tokens[1:] = lax.optimization_barrier((column, *quad_tokens[1:]))
+
+    gate_up = jnp.concatenate([w_gate[0], w_up[0]], axis=1)
+    gate_up_chip = lax.ppermute(gate_up, "head", CHIP_SWAP)
+    down_chip = lax.ppermute(w_down[0], "head", CHIP_SWAP)
+    gate_up_quad = quad_of(gate_up, gate_up_chip)
+    down_quad = quad_of(w_down[0], down_chip)
+
     own = spread_over(column, "blk", X_GROUPS).reshape(N_X, LAT + ROPE, N_Y * HALF)
-    own, *proj[4:] = lax.optimization_barrier((own, *proj[4:]))
     other = lax.ppermute(own, "head", CORE_SWAP)
 
     place = jnp.stack([blk, core, lax.axis_index("head") & (QUAD - 1)]).astype(jnp.int32)
     lifted = attend(place, queries, own, other, value_up)
 
     lifted_row = lax.all_to_all(
-        lifted, "blk", 0, 0, tiled=True, axis_index_groups=X_GROUPS
-    ).reshape(N_X * TOK, lifted.shape[2])
-    partial = project(place, lifted_row, proj)
-    spread = lax.all_to_all(
-        partial, ("blk", "head"), 0, 0, tiled=True, axis_index_groups=XH_GROUPS
-    )
-    summed = jnp.sum(spread.reshape(N_X, N_HEAD, HALF, 128).astype(jnp.float32), axis=1)
-    keep = lax.dynamic_slice(summed, (2 * core, 0, 0), (2, HALF, 128))
-    send = lax.dynamic_slice(summed, (2 - 2 * core, 0, 0), (2, HALF, 128))
-    got = lax.ppermute(send, "head", CORE_SWAP)
-    top = jnp.where(core == 0, keep, got)
-    bottom = jnp.where(core == 0, got, keep)
-    attended = jnp.concatenate([top, bottom], axis=1)
-    attended = jnp.concatenate([attended[0], attended[1]], axis=1)
-    mid_state = (tokens.astype(jnp.float32) + attended).astype(jnp.bfloat16)
+        lifted, ("blk", "head"), 0, 0, tiled=True, axis_index_groups=XC_GROUPS
+    )
+    partial = project(lifted_row, proj)
+    spread = lax.all_to_all(partial, ("blk", "head"), 0, 0, tiled=True, axis_index_groups=XZ_GROUPS)
+    summed = jnp.sum(spread.reshape(N_X, N_Z, HALF, 128).astype(jnp.float32), axis=1)
+    attended = spread_over(summed, "head", QUADS).reshape(QUAD, N_X, HALF, 128)
+    mid_quad, mid_state = middle(place, attended, quad_tokens)
     mid_wide = mid_state.astype(jnp.float32)
 
     row_count = tokens.shape[0]
@@ -270,8 +323,11 @@
     ranks = jnp.sum(earlier * onehot_ids, axis=1)
     slot_ids = flat_ids * CAP + ranks
     slot_hits = jnp.arange(SLOTS, dtype=jnp.int32)[:, None] == slot_ids[None, :]
+    row_ids = jnp.arange(ROWS, dtype=jnp.int32)
+    row_slots = row_ids // PART * CAP + place[2] * PART + row_ids % PART
+    row_hits = row_slots[:, None] == slot_ids[None, :]
     select = jnp.sum(
-        slot_hits.astype(jnp.bfloat16).reshape(SLOTS, row_count, choose_count), axis=2
+        row_hits.astype(jnp.bfloat16).reshape(ROWS, row_count, choose_count), axis=2
     )
     combine = jnp.sum(
         jnp.where(slot_hits, expert_gates.reshape(-1)[None, :], 0.0).reshape(
@@ -281,20 +337,16 @@
     )
 
     outgoing = (
-        jnp.dot(select, mid_state, preferred_element_type=jnp.float32)
+        jnp.dot(select, mid_quad, preferred_element_type=jnp.float32)
         .astype(jnp.bfloat16)
-        .reshape(N_BLK * QUAD, PART * 2, 128)
-    )
-    incoming = lax.all_to_all(
-        outgoing, ("blk", "head"), 0, 0, tiled=True, axis_index_groups=BLK_QUAD
-    )
-    rows_here = (
-        incoming.reshape(N_BLK, QUAD, PART, 256).transpose(0, 2, 1, 3).reshape(ROWS, QUAD * 256)
-    )
+        .reshape(N_BLK, PART * QUAD * 2, 128)
+    )
+    incoming = lax.all_to_all(outgoing, "blk", 0, 0, tiled=True)
+    rows_here = incoming.reshape(ROWS, QUAD * 256)
     rows = spread_over(rows_here, "head", ACROSS).reshape(QUAD, ROWS, QUAD * 256)
-    act = hidden(place, rows, quad_weights)
+    act = hidden(place, rows, gate_up_quad)
     acts = lax.all_to_all(act, "head", 0, 0, tiled=True, axis_index_groups=ACROSS)
-    expert_out = down(place, acts, quad_weights)
+    expert_out = down(place, acts, down_quad)
     sent = (
         expert_out.reshape(N_BLK, PART, QUAD, 256)
         .transpose(0, 2, 1, 3)
@@ -321,6 +373,7 @@
         P("blk", None, "head"),
         P("blk", None, "head"),
     )
+
     return jax.shard_map(
         per_device, mesh=mesh, in_specs=placed, out_specs=P("blk", "head"), check_vma=False
     )

time: 275 us -> 304 us (1.11)
  waiting for transfers between devices: 92.5 us -> 162 us
  blocking collectives: 63.2 us -> 0 us
  between operations: 0.43 us -> 13.8 us
  starting transfers between devices: 75.1 us -> 85.5 us
    all_to_all x3 -> x0, blocking collectives: 63.2 us -> none  [the longest x1 28 us: per_device(): lax.all_to_all(outgoing, ('blk', 'head'), 0, 0, tiled=True, axis_index_gr...]
    ppermute x11 -> x10, waiting for transfers between devices: 19.2 us -> 47.6 us  [the longest x1 45.1 us: per_device(): down_chip = lax.ppermute(w_down[0], 'head', CHIP_SWAP)]
    all_to_all x0 -> x3, waiting for transfers between devices: none -> 26.7 us  [the longest x1 17.9 us: per_device(): lax.all_to_all(act, 'head', 0, 0, tiled=True, axis_index_groups=ACROSS)]
    all_gather x0 -> x1, waiting for transfers between devices: none -> 25.7 us  [per_device(): lax.all_gather(moved, 'blk', axis=0, tiled=True, axis_index_groups=Y_GROUPS)]
    all_to_all x0 -> x3, starting transfers between devices: none -> 17.9 us  [the longest x1 7.79 us: per_device(): incoming = lax.all_to_all(outgoing, 'blk', 0, 0, tiled=True)]
    ppermute x11 -> x10, starting transfers between devices: 36.8 us -> 23.3 us  [the longest x3 7.58 us: per_device(): lax.ppermute(tokens, 'head', swap)]
    all_to_all x3 -> x4, waiting for transfers between devices: 30.6 us -> 20.6 us  [spread_over(): lax.all_to_all(jnp.broadcast_to(x[None], (count,) + x.shape), axis, 0, 0,...]
    all_to_all x3 -> x4, starting transfers between devices: 17.7 us -> 21.6 us  [spread_over(): lax.all_to_all(jnp.broadcast_to(x[None], (count,) + x.shape), axis, 0, 0,...]
  transfers between devices with their start and end apart: 17 -> 21, of which waited for: 9 -> 12; matrix products, arithmetic and copies ran while one was open for 5% -> 3% of each run, Pallas kernels for 3% -> 5%
where the time goes in v3:
time: 304 us; the launch traced here: 303 us
  waiting for transfers between devices  162 us (53%)
  starting transfers between devices  85.5 us (28%)
  Pallas kernels  21.2 us (7%)
  local copies, waits for them, and re-layouts  14.5 us (5%)
  between operations  13.8 us (5%)
  other arithmetic  4.53 us (1%)
    ppermute x1, waiting for transfers between devices, per_device(): down_chip = lax.ppermute(w_down[0], 'head', CHIP_SWAP)  45.1 us
    all_gather x1, waiting for transfers between devices, per_device(): lax.all_gather(moved, 'blk', axis=0, tiled=True, axis_index_groups=Y_GROUPS)  25.7 us
    all_to_all x4, starting transfers between devices, spread_over(): lax.all_to_all(jnp.broadcast_to(x[None], (count,) + x.shape), axis, 0, 0,...  21.6 us
    all_to_all x4, waiting for transfers between devices, spread_over(): lax.all_to_all(jnp.broadcast_to(x[None], (count,) + x.shape), axis, 0, 0,...  20.6 us
    all_to_all x1, waiting for transfers between devices, per_device(): lax.all_to_all(partial, ('blk', 'head'), 0, 0, tiled=True, axis_index_gro...  20.5 us
    all_to_all x1, waiting for transfers between devices, per_device(): lax.all_to_all(sent, ('blk', 'head'), 0, 0, tiled=True, axis_index_groups...  19.1 us
    all_to_all x1, waiting for transfers between devices, per_device(): lax.all_to_all(act, 'head', 0, 0, tiled=True, axis_index_groups=ACROSS)  17.9 us
    all_to_all x1, starting transfers between devices, per_device(): lax.all_to_all(sent, ('blk', 'head'), 0, 0, tiled=True, axis_index_groups...  10.6 us
  transfers between devices with their start and end apart: 21, of which 12 were waited for; matrix products, arithmetic and copies ran while one was open for 3% of the time, Pallas kernels for 5%

profile of v3, /device:TPU:8, one launch (start us, length us, event | category | flops | bytes accessed | tf_op | source)
XLA Modules:
  0.0 303.1 jit_solution(12001397315645271222)
XLA Ops:
  8.2 9.1 %all-to-all-start = ((bf16[8,32,576]{2,1,0:T(8,128)(2,1)}), bf16[8,32,576]{2,1,0:T(8,128)(2,1)S(1)}, u32[]{:S(2)}, u32[]{:S(2)}) async-start(bf16[8,32,576]{2,1,0:T(8,128)(2,1)} %broadcast_in_dim.18), calls=%async_computation | async-start | bytes 655360 | tf_op jit(solution)/shard_map/all_to_all | solution.py:267
  19.2 2.7 collective-permute-start.1
  21.9 3.0 collective-permute-start.2
  28.9 4.3 %all-to-all-start.1 = ((bf16[4,576,256]{2,1,0:T(8,128)(2,1)}), bf16[4,576,256]{2,1,0:T(8,128)(2,1)S(1)}, u32[]{:S(2)}, u32[]{:S(2)}) async-start(bf16[4,576,256]{2,1,0:T(8,128)(2,1)} %broadcast_in_dim.19), calls=%async_computation.1 | async-start | bytes 2359296 | tf_op jit(solution)/shard_map/all_to_all | solution.py:267
  35.1 14.9 %all-to-all-done.1.own_ref = bf16[4,576,256]{2,1,0:T(8,128)(2,1)S(1)} async-done(((bf16[4,576,256]{2,1,0:T(8,128)(2,1)}), bf16[4,576,256]{2,1,0:T(8,128)(2,1)S(1)}, u32[]{:S(2)}, u32[]{:S(2)}) %all-to-all-start.1) | async-done | bytes 1179680 | tf_op jit(solution)/shard_map/all_to_all | solution.py:267
  55.7 5.0 %attend.1 = bf16[8,64,512]{2,1,0:T(8,128)(2,1)} custom-call(s32[3]{0:T(128)} %pad_add_fusion.place_ref, bf16[64,2304]{1,0:T(8,128)(2,1)} %q_ref.1, bf16[4,576,256]{2,1,0:T(8,128)(2,1)} %copy-done.3, bf16[4,576,256]{2,1,0:T(8,128)(2,1)} %copy-done.6, bf16[4,512,128]{2,1,0:T(8,128)(2,1)} %lift_ref.1), custom_call_target="tpu_custom_call" | custom-call | tf_op jit(solution)/shard_map/attend/pallas_call | solution.py:200
  60.7 3.5 %all-to-all-start.2 = ((bf16[8,64,512]{2,1,0:T(8,128)(2,1)}), bf16[8,64,512]{2,1,0:T(8,128)(2,1)S(1)}, u32[]{:S(2)}, u32[]{:S(2)}) async-start(bf16[8,64,512]{2,1,0:T(8,128)(2,1)} %attend.1), calls=%async_computation.2 | async-start | bytes 1048576 | tf_op jit(solution)/shard_map/all_to_all | solution.py:306
  66.0 3.0 collective-permute-start.6
  69.0 25.7 %all-gather.2.cloned.1.call-done = bf16[4096,128]{1,0:T(8,128)(2,1)} async-done(((bf16[512,128]{1,0:T(8,128)(2,1)}), bf16[4096,128]{1,0:T(8,128)(2,1)}) %all-gather.2.cloned.1.call-update) | async-done | bytes 1048592 | tf_op jit(solution)/shard_map/all_gather | solution.py:287
  98.0 10.2 %all-to-all-start.3 = ((bf16[32,32,128]{2,1,0:T(8,128)(2,1)}), bf16[32,32,128]{2,1,0:T(8,128)(2,1)S(1)}, u32[]{:S(2)}, u32[]{:S(2)}) async-start(bf16[32,32,128]{2,1,0:T(8,128)(2,1)} %project.1), calls=%async_computation.3 | async-start | bytes 524288 | tf_op jit(solution)/shard_map/all_to_all | solution.py:310
  110.2 20.5 %all-to-all-done.3 = bf16[32,32,128]{2,1,0:T(8,128)(2,1)S(1)} async-done(((bf16[32,32,128]{2,1,0:T(8,128)(2,1)}), bf16[32,32,128]{2,1,0:T(8,128)(2,1)S(1)}, u32[]{:S(2)}, u32[]{:S(2)}) %all-to-all-start.3) | async-done | bytes 262176 | tf_op jit(solution)/shard_map/all_to_all | solution.py:310
  131.5 3.4 %all-to-all-start.4 = ((f32[4,4,32,128]{3,2,1,0:T(8,128)}), f32[4,4,32,128]{3,2,1,0:T(8,128)S(1)}, u32[]{:S(2)}, u32[]{:S(2)}) async-start(f32[4,4,32,128]{3,2,1,0:T(8,128)} %broadcast_in_dim.20), calls=%async_computation.4 | async-start | bytes 524288 | tf_op jit(solution)/shard_map/all_to_all | solution.py:267
  135.3 5.6 %all-to-all-done.4.attended_ref = f32[4,4,32,128]{3,2,1,0:T(8,128)S(1)} async-done(((f32[4,4,32,128]{3,2,1,0:T(8,128)}), f32[4,4,32,128]{3,2,1,0:T(8,128)S(1)}, u32[]{:S(2)}, u32[]{:S(2)}) %all-to-all-start.4) | async-done | bytes 262176 | tf_op jit(solution)/shard_map/all_to_all | solution.py:267
  145.5 7.8 %all-to-all-start.5 = ((bf16[32,40,128]{2,1,0:T(8,128)(2,1)}), bf16[32,40,128]{2,1,0:T(8,128)(2,1)S(1)}, u32[]{:S(2)}, u32[]{:S(2)}) async-start(bf16[32,40,128]{2,1,0:T(8,128)(2,1)} %reshape.100), calls=%async_computation.5 | async-start | bytes 655360 | tf_op jit(solution)/shard_map/all_to_all | solution.py:344
  157.7 8.8 %all-to-all-done.5 = bf16[32,40,128]{2,1,0:T(8,128)(2,1)S(1)} async-done(((bf16[32,40,128]{2,1,0:T(8,128)(2,1)}), bf16[32,40,128]{2,1,0:T(8,128)(2,1)S(1)}, u32[]{:S(2)}, u32[]{:S(2)}) %all-to-all-start.5) | async-done | bytes 327712 | tf_op jit(solution)/shard_map/all_to_all | solution.py:344
  167.8 4.8 %all-to-all-start.6 = ((bf16[4,160,1024]{2,1,0:T(8,128)(2,1)}), bf16[4,160,1024]{2,1,0:T(8,128)(2,1)S(1)}, u32[]{:S(2)}, u32[]{:S(2)}) async-start(bf16[4,160,1024]{2,1,0:T(8,128)(2,1)} %broadcast_in_dim.48), calls=%async_computation.6 | async-start | bytes 2621440 | tf_op jit(solution)/shard_map/all_to_all | solution.py:267
  172.6 2.7 collective-permute-start.9
  177.2 45.1 %collective-permute-done.9.refs_2_ = bf16[2048,256]{1,0:T(8,128)(2,1)} collective-permute-done((bf16[2048,256]{1,0:T(8,128)(2,1)}, bf16[2048,256]{1,0:T(8,128)(2,1)}, u32[]{:S(2)}, u32[]{:S(2)}) %collective-permute-start.9) | collective-permute-done | bytes 1048608 | tf_op jit(solution)/shard_map/ppermute | solution.py:296
  225.4 6.7 %hidden.1 = bf16[4,160,512]{2,1,0:T(8,128)(2,1)} custom-call(s32[3]{0:T(128)} %pad_add_fusion.place_ref, bf16[4,160,1024]{2,1,0:T(8,128)(2,1)} %copy-done.2, bf16[4096,256]{1,0:T(8,128)(2,1)} %copy-done.1, bf16[4096,256]{1,0:T(8,128)(2,1)} %collective-permute-done.5.refs_1_, bf16[4096,256]{1,0:T(8,128)(2,1)} %collective-permute-done.6.refs_2_, ...), custom_call_target="tpu_custom_call" | custom-call | tf_op jit(solution)/shard_map/hidden/pallas_call | solution.py:236
  232.1 6.6 %all-to-all-start.7 = ((bf16[4,160,512]{2,1,0:T(8,128)(2,1)}), bf16[4,160,512]{2,1,0:T(8,128)(2,1)S(1)}, u32[]{:S(2)}, u32[]{:S(2)}) async-start(bf16[4,160,512]{2,1,0:T(8,128)(2,1)} %hidden.1), calls=%async_computation.7 | async-start | bytes 1310720 | tf_op jit(solution)/shard_map/all_to_all | solution.py:348
  238.7 17.9 %all-to-all-done.7.act_ref = bf16[4,160,512]{2,1,0:T(8,128)(2,1)S(1)} async-done(((bf16[4,160,512]{2,1,0:T(8,128)(2,1)}), bf16[4,160,512]{2,1,0:T(8,128)(2,1)S(1)}, u32[]{:S(2)}, u32[]{:S(2)}) %all-to-all-start.7) | async-done | bytes 655392 | tf_op jit(solution)/shard_map/all_to_all | solution.py:348
  257.5 5.1 %down.1 = bf16[160,1024]{1,0:T(8,128)(2,1)} custom-call(s32[3]{0:T(128)} %pad_add_fusion.place_ref, bf16[4,160,512]{2,1,0:T(8,128)(2,1)} %copy-done.4, bf16[2048,256]{1,0:T(8,128)(2,1)} %bitcast.46, bf16[2048,256]{1,0:T(8,128)(2,1)} %collective-permute-done.8.refs_1_, bf16[2048,256]{1,0:T(8,128)(2,1)} %collective-permute-done.9.refs_2_, ...), custom_call_target="tpu_custom_call" | custom-call | tf_op jit(solution)/shard_map/down/pallas_call | solution.py:255
  264.9 10.6 %all-to-all-start.8 = ((bf16[128,10,128]{2,1,0:T(8,128)(2,1)}), bf16[128,10,128]{2,1,0:T(8,128)(2,1)S(1)}, u32[]{:S(2)}, u32[]{:S(2)}) async-start(bf16[128,10,128]{2,1,0:T(8,128)(2,1)} %reshape.102), calls=%async_computation.8 | async-start | bytes 1048576 | tf_op jit(solution)/shard_map/all_to_all | solution.py:355
  276.0 19.1 %all-to-all-done.8 = bf16[128,10,128]{2,1,0:T(8,128)(2,1)S(1)} async-done(((bf16[128,10,128]{2,1,0:T(8,128)(2,1)}), bf16[128,10,128]{2,1,0:T(8,128)(2,1)S(1)}, u32[]{:S(2)}, u32[]{:S(2)}) %all-to-all-start.8) | async-done | bytes 327712 | tf_op jit(solution)/shard_map/all_to_all | solution.py:355
  (90 shorter events, 43.4 us)
Async XLA Ops:
  8.2 19.4 %all-to-all-start = ((bf16[8,32,576]{2,1,0:T(8,128)(2,1)}), bf16[8,32,576]{2,1,0:T(8,128)(2,1)S(1)}, u32[]{:S(2)}, u32[]{:S(2)}) async-start(bf16[8,32,576]{2,1,0:T(8,128)(2,1)} %broadcast_in_dim.18), calls=%async_computation | async-start | bytes 655360 | tf_op jit(solution)/shard_map/all_to_all | solution.py:267
  17.3 7.6 %collective-permute-start = (bf16[64,256]{1,0:T(8,128)(2,1)}, bf16[64,256]{1,0:T(8,128)(2,1)S(1)}, u32[]{:S(2)}, u32[]{:S(2)}) collective-permute-start(bf16[64,256]{1,0:T(8,128)(2,1)} %refs_0_.1), channel_id=1, source_target_pairs={{0,1},{1,0},{2,3},{3,2},{4,5},{5,4},{6,7},{7,6},{8,9},{9,8},{10,11... | collective-permute-start | bytes 98312 | tf_op jit(solution)/shard_map/ppermute | solution.py:284
  19.2 6.0 %collective-permute-start.1 = (bf16[64,256]{1,0:T(8,128)(2,1)}, bf16[64,256]{1,0:T(8,128)(2,1)S(1)}, u32[]{:S(2)}, u32[]{:S(2)}) collective-permute-start(bf16[64,256]{1,0:T(8,128)(2,1)} %refs_0_.1), channel_id=1, source_target_pairs={{0,2},{1,3},{2,0},{3,1},{4,6},{5,7},{6,4},{7,5},{8,10},{9,11},{10,... | collective-permute-start | bytes 98312 | tf_op jit(solution)/shard_map/ppermute | solution.py:284
  21.9 5.4 %collective-permute-start.2 = (bf16[64,256]{1,0:T(8,128)(2,1)}, bf16[64,256]{1,0:T(8,128)(2,1)S(1)}, u32[]{:S(2)}, u32[]{:S(2)}) collective-permute-start(bf16[64,256]{1,0:T(8,128)(2,1)} %refs_0_.1), channel_id=1, source_target_pairs={{0,3},{1,2},{2,1},{3,0},{4,7},{5,6},{6,5},{7,4},{8,11},{9,10},{10,... | collective-permute-start | bytes 98312 | tf_op jit(solution)/shard_map/ppermute | solution.py:284
  28.9 21.1 %all-to-all-start.1 = ((bf16[4,576,256]{2,1,0:T(8,128)(2,1)}), bf16[4,576,256]{2,1,0:T(8,128)(2,1)S(1)}, u32[]{:S(2)}, u32[]{:S(2)}) async-start(bf16[4,576,256]{2,1,0:T(8,128)(2,1)} %broadcast_in_dim.19), calls=%async_computation.1 | async-start | bytes 2359296 | tf_op jit(solution)/shard_map/all_to_all | solution.py:267
  33.2 61.5 %all-gather.2.cloned.1.call-start = ((), (), s32[]{:S(2)}) async-start(), calls=%async_computation.9 | async-start | bytes 1179648 | tf_op jit(solution)/shard_map/all_gather | solution.py:287
  33.2 18.7 %collective-permute-start.4 = (bf16[512,128]{1,0:T(8,128)(2,1)S(1)}, bf16[512,128]{1,0:T(8,128)(2,1)S(1)}, u32[]{:S(2)}, u32[]{:S(2)}) collective-permute-start(bf16[512,128]{1,0:T(8,128)(2,1)S(1)} %copy-done.15), channel_id=1, source_target_pairs={{0,0},{1,64},{2,2},{3,66},{4,4},{5,68},{6,6},{7,70},{8,8},{9,72},{... | collective-permute-start | bytes 393224 | tf_op jit(solution)/shard_map/ppermute | solution.py:286
  49.9 4.7 %collective-permute-start.3 = (bf16[4,576,256]{2,1,0:T(8,128)(2,1)S(1)}, bf16[4,576,256]{2,1,0:T(8,128)(2,1)S(1)}, u32[]{:S(2)}, u32[]{:S(2)}) collective-permute-start(bf16[4,576,256]{2,1,0:T(8,128)(2,1)S(1)} %all-to-all-done.1.own_ref), channel_id=1, source_target_pairs={{0,1},{1,0},{2,3},{3,2},{4,5},{5,4},{6,7},{7,6},{8,9},{9,8},{10,11... | collective-permute-start | bytes 3538952 | tf_op jit(solution)/shard_map/ppermute | solution.py:301
  60.7 34.0 %all-to-all-start.2 = ((bf16[8,64,512]{2,1,0:T(8,128)(2,1)}), bf16[8,64,512]{2,1,0:T(8,128)(2,1)S(1)}, u32[]{:S(2)}, u32[]{:S(2)}) async-start(bf16[8,64,512]{2,1,0:T(8,128)(2,1)} %attend.1), calls=%async_computation.2 | async-start | bytes 1048576 | tf_op jit(solution)/shard_map/all_to_all | solution.py:306
  66.0 87.3 %copy-start.1 = (bf16[4096,256]{1,0:T(8,128)(2,1)}, bf16[4096,256]{1,0:T(8,128)(2,1)S(1)}, u32[]{:S(2)}) copy-start(bf16[4096,256]{1,0:T(8,128)(2,1)S(1)} %pad_maximum_fusion.refs_0_) | copy-start | bytes 6291460
  66.0 42.2 %copy-start.13 = (s32[64,8]{0,1:T(8,128)S(1)}, s32[64,8]{0,1:T(8,128)}, u32[]{:S(2)}) copy-start(s32[64,8]{0,1:T(8,128)} %param.15) | copy-start | bytes 6148
  66.0 89.2 %collective-permute-start.6 = (bf16[4096,256]{1,0:T(8,128)(2,1)S(1)}, bf16[4096,256]{1,0:T(8,128)(2,1)}, u32[]{:S(2)}, u32[]{:S(2)}) collective-permute-start(bf16[4096,256]{1,0:T(8,128)(2,1)S(1)} %pad_maximum_fusion.refs_0_), channel_id=1, source_target_pairs={{0,2},{1,3},{2,0},{3,1},{4,6},{5,7},{6,4},{7,5},{8,10},{9,11},{10,... | collective-permute-start | bytes 6291464 | tf_op jit(solution)/shard_map/ppermute | solution.py:295
  98.0 32.7 %all-to-all-start.3 = ((bf16[32,32,128]{2,1,0:T(8,128)(2,1)}), bf16[32,32,128]{2,1,0:T(8,128)(2,1)S(1)}, u32[]{:S(2)}, u32[]{:S(2)}) async-start(bf16[32,32,128]{2,1,0:T(8,128)(2,1)} %project.1), calls=%async_computation.3 | async-start | bytes 524288 | tf_op jit(solution)/shard_map/all_to_all | solution.py:310
  131.5 9.4 %all-to-all-start.4 = ((f32[4,4,32,128]{3,2,1,0:T(8,128)}), f32[4,4,32,128]{3,2,1,0:T(8,128)S(1)}, u32[]{:S(2)}, u32[]{:S(2)}) async-start(f32[4,4,32,128]{3,2,1,0:T(8,128)} %broadcast_in_dim.20), calls=%async_computation.4 | async-start | bytes 524288 | tf_op jit(solution)/shard_map/all_to_all | solution.py:267
  145.5 20.9 %all-to-all-start.5 = ((bf16[32,40,128]{2,1,0:T(8,128)(2,1)}), bf16[32,40,128]{2,1,0:T(8,128)(2,1)S(1)}, u32[]{:S(2)}, u32[]{:S(2)}) async-start(bf16[32,40,128]{2,1,0:T(8,128)(2,1)} %reshape.100), calls=%async_computation.5 | async-start | bytes 655360 | tf_op jit(solution)/shard_map/all_to_all | solution.py:344
  153.3 71.0 %collective-permute-start.5 = (bf16[4096,256]{1,0:T(8,128)(2,1)S(1)}, bf16[4096,256]{1,0:T(8,128)(2,1)}, u32[]{:S(2)}, u32[]{:S(2)}) collective-permute-start(bf16[4096,256]{1,0:T(8,128)(2,1)S(1)} %pad_maximum_fusion.refs_0_), channel_id=1, source_target_pairs={{0,1},{1,0},{2,3},{3,2},{4,5},{5,4},{6,7},{7,6},{8,9},{9,8},{10,11... | collective-permute-start | bytes 6291464 | tf_op jit(solution)/shard_map/ppermute | solution.py:273
  155.2 69.0 %collective-permute-start.7 = (bf16[4096,256]{1,0:T(8,128)(2,1)}, bf16[4096,256]{1,0:T(8,128)(2,1)}, u32[]{:S(2)}, u32[]{:S(2)}) collective-permute-start(bf16[4096,256]{1,0:T(8,128)(2,1)} %collective-permute-done.6.refs_2_), channel_id=1, source_target_pairs={{0,1},{1,0},{2,3},{3,2},{4,5},{5,4},{6,7},{7,6},{8,9},{9,8},{10,11... | collective-permute-start | bytes 6291464 | tf_op jit(solution)/shard_map/ppermute | solution.py:274
  167.8 56.5 %all-to-all-start.6 = ((bf16[4,160,1024]{2,1,0:T(8,128)(2,1)}), bf16[4,160,1024]{2,1,0:T(8,128)(2,1)S(1)}, u32[]{:S(2)}, u32[]{:S(2)}) async-start(bf16[4,160,1024]{2,1,0:T(8,128)(2,1)} %broadcast_in_dim.48), calls=%async_computation.6 | async-start | bytes 2621440 | tf_op jit(solution)/shard_map/all_to_all | solution.py:267
  172.6 49.7 %collective-permute-start.9 = (bf16[2048,256]{1,0:T(8,128)(2,1)}, bf16[2048,256]{1,0:T(8,128)(2,1)}, u32[]{:S(2)}, u32[]{:S(2)}) collective-permute-start(bf16[2048,256]{1,0:T(8,128)(2,1)} %bitcast.44), channel_id=1, source_target_pairs={{0,2},{1,3},{2,0},{3,1},{4,6},{5,7},{6,4},{7,5},{8,10},{9,11},{10,... | collective-permute-start | bytes 3145736 | tf_op jit(solution)/shard_map/ppermute | solution.py:296
  175.3 63.4 %collective-permute-start.8 = (bf16[2048,256]{1,0:T(8,128)(2,1)}, bf16[2048,256]{1,0:T(8,128)(2,1)}, u32[]{:S(2)}, u32[]{:S(2)}) collective-permute-start(bf16[2048,256]{1,0:T(8,128)(2,1)} %bitcast.45), channel_id=1, source_target_pairs={{0,1},{1,0},{2,3},{3,2},{4,5},{5,4},{6,7},{7,6},{8,9},{9,8},{10,11... | collective-permute-start | bytes 3145736 | tf_op jit(solution)/shard_map/ppermute | solution.py:273
  222.4 16.4 %collective-permute-start.10 = (bf16[2048,256]{1,0:T(8,128)(2,1)}, bf16[2048,256]{1,0:T(8,128)(2,1)}, u32[]{:S(2)}, u32[]{:S(2)}) collective-permute-start(bf16[2048,256]{1,0:T(8,128)(2,1)} %collective-permute-done.9.refs_2_), channel_id=1, source_target_pairs={{0,1},{1,0},{2,3},{3,2},{4,5},{5,4},{6,7},{7,6},{8,9},{9,8},{10,11... | collective-permute-start | bytes 3145736 | tf_op jit(solution)/shard_map/ppermute | solution.py:274
  232.1 24.5 %all-to-all-start.7 = ((bf16[4,160,512]{2,1,0:T(8,128)(2,1)}), bf16[4,160,512]{2,1,0:T(8,128)(2,1)S(1)}, u32[]{:S(2)}, u32[]{:S(2)}) async-start(bf16[4,160,512]{2,1,0:T(8,128)(2,1)} %hidden.1), calls=%async_computation.7 | async-start | bytes 1310720 | tf_op jit(solution)/shard_map/all_to_all | solution.py:348
  263.8 31.6 %copy-start.12 = (bf16[64,256]{1,0:T(8,128)(2,1)S(1)}, bf16[64,256]{1,0:T(8,128)(2,1)}, u32[]{:S(2)}) copy-start(bf16[64,256]{1,0:T(8,128)(2,1)} %get-tuple-element.15) | copy-start | bytes 98308
  264.9 30.3 %all-to-all-start.8 = ((bf16[128,10,128]{2,1,0:T(8,128)(2,1)}), bf16[128,10,128]{2,1,0:T(8,128)(2,1)S(1)}, u32[]{:S(2)}, u32[]{:S(2)}) async-start(bf16[128,10,128]{2,1,0:T(8,128)(2,1)} %reshape.102), calls=%async_computation.8 | async-start | bytes 1048576 | tf_op jit(solution)/shard_map/all_to_all | solution.py:355
  (13 other events, 38.3 us)
Sparse Core Ops, SparseCore 0:
  52.7 41.9 all-gather.1

commit v4 on v3

--- a/solution.py
+++ b/solution.py
@@ -60,7 +60,6 @@
 ]
 CORE_SWAP = [(i, i ^ 1) for i in range(N_HEAD)]
 CHIP_SWAP = [(i, i ^ 2) for i in range(N_HEAD)]
-BOTH_SWAP = [(i, i ^ 3) for i in range(N_HEAD)]
 
 
 def attention_kernel(place_ref, q_ref, own_ref, other_ref, lift_ref, out_ref):
@@ -126,28 +125,21 @@
                     ]
 
 
-def mid_kernel(place_ref, attended_ref, *refs):
-    token_refs, (quad_ref, own_ref) = refs[:QUAD], refs[QUAD:]
-    me = place_ref[2]
-    for j in range(QUAD):
-        owner = jnp.bitwise_xor(me, j)
-        core = owner // 2
-        first = (owner % 2) * 2
+def mid_kernel(place_ref, shared_ref, quad_ref, own_ref):
+    for i in range(QUAD):
+        parts = []
         for p in range(2):
-            rows = slice(p * HALF, (p + 1) * HALF)
             wide = [
-                token_refs[j][rows, i * 128 : (i + 1) * 128].astype(jnp.float32)
-                + attended_ref[p * 2 + core, first + i]
-                for i in range(2)
+                shared_ref[i, 4 + f * 2 + p] + shared_ref[p * 2 + i // 2, i % 2 * 2 + f]
+                for f in range(2)
             ]
-            mid = jnp.concatenate(wide, axis=1).astype(jnp.bfloat16)
-            if j == 0:
-                own_ref[rows, :] = mid
-            for other in range(QUAD):
-
-                @pl.when(owner == other)
-                def _():
-                    quad_ref[rows, other * 256 : (other + 1) * 256] = mid
+            parts.append(jnp.concatenate(wide, axis=1))
+        mid = jnp.concatenate(parts, axis=0).astype(jnp.bfloat16)
+        quad_ref[:, i * 256 : (i + 1) * 256] = mid
+
+        @pl.when(place_ref[2] == i)
+        def _():
+            own_ref[...] = mid
 
 
 def hidden_kernel(place_ref, rows_ref, *refs):
@@ -217,18 +209,20 @@
     )(lifted, proj)
 
 
-def middle(place, attended, tokens):
+def middle(place, shared):
     return pl.pallas_call(
         mid_kernel,
         out_shape=(
             jax.ShapeDtypeStruct((TOK, QUAD * 256), jnp.bfloat16),
             jax.ShapeDtypeStruct((TOK, 256), jnp.bfloat16),
         ),
-        in_specs=[pl.BlockSpec(memory_space=pltpu.SMEM)]
-        + [pl.BlockSpec(memory_space=pltpu.VMEM)] * (1 + QUAD),
+        in_specs=[
+            pl.BlockSpec(memory_space=pltpu.SMEM),
+            pl.BlockSpec(memory_space=pltpu.VMEM),
+        ],
         out_specs=(pl.BlockSpec(memory_space=pltpu.VMEM),) * 2,
         name="middle",
-    )(place, attended, *tokens)
+    )(place, shared)
 
 
 def hidden(place, rows, weights):
@@ -280,16 +274,12 @@
     blk = lax.axis_index("blk")
     core = lax.axis_index("head") & 1
 
-    quad_tokens = [tokens] + [
-        lax.ppermute(tokens, "head", swap) for swap in (CORE_SWAP, CHIP_SWAP, BOTH_SWAP)
-    ]
     moved = lax.ppermute(out_proj, ("blk", "head"), PROJ_MOVE)
     proj = lax.all_gather(moved, "blk", axis=0, tiled=True, axis_index_groups=Y_GROUPS)
     proj = proj.reshape(N_Y // 2, 2 * out_proj.shape[0], 128)
 
     half = lax.dynamic_slice(latents, (core * HALF, 0), (HALF, LAT + ROPE))
     column = spread_over(half, "blk", Y_GROUPS).reshape(N_Y * HALF, LAT + ROPE).T
-    column, *quad_tokens[1:] = lax.optimization_barrier((column, *quad_tokens[1:]))
 
     gate_up = jnp.concatenate([w_gate[0], w_up[0]], axis=1)
     gate_up_chip = lax.ppermute(gate_up, "head", CHIP_SWAP)
@@ -309,8 +299,10 @@
     partial = project(lifted_row, proj)
     spread = lax.all_to_all(partial, ("blk", "head"), 0, 0, tiled=True, axis_index_groups=XZ_GROUPS)
     summed = jnp.sum(spread.reshape(N_X, N_Z, HALF, 128).astype(jnp.float32), axis=1)
-    attended = spread_over(summed, "head", QUADS).reshape(QUAD, N_X, HALF, 128)
-    mid_quad, mid_state = middle(place, attended, quad_tokens)
+    token_blocks = jnp.stack([tokens[:, :128], tokens[:, 128:]]).reshape(4, HALF, 128)
+    shared = jnp.concatenate([summed, token_blocks.astype(jnp.float32)], axis=0)
+    shared = spread_over(shared, "head", QUADS).reshape(QUAD, 8, HALF, 128)
+    mid_quad, mid_state = middle(place, shared)
     mid_wide = mid_state.astype(jnp.float32)
 
     row_count = tokens.shape[0]

time: 304 us -> 311 us (1.023)
  blocking collectives: 0 us -> 19.2 us
  starting transfers between devices: 85.5 us -> 69 us
  waiting for transfers between devices: 162 us -> 166 us
    all_to_all x4 -> x3, waiting for transfers between devices: 20.6 us -> 42.2 us  [spread_over(): lax.all_to_all(jnp.broadcast_to(x[None], (count,) + x.shape), axis, 0, 0,...]
    all_to_all x0 -> x1, blocking collectives: none -> 19.2 us  [spread_over(): lax.all_to_all(jnp.broadcast_to(x[None], (count,) + x.shape), axis, 0, 0,...]
    all_to_all x1, waiting for transfers between devices: 20.5 us -> 6.75 us  [per_device(): lax.all_to_all(partial, ('blk', 'head'), 0, 0, tiled=True, axis_index_gro...]
    ppermute x3 -> x0, starting transfers between devices: 7.58 us -> none  [per_device(): lax.ppermute(tokens, 'head', swap)]
    all_to_all x4 -> x3, starting transfers between devices: 21.6 us -> 14.4 us  [spread_over(): lax.all_to_all(jnp.broadcast_to(x[None], (count,) + x.shape), axis, 0, 0,...]
    all_gather x1, waiting for transfers between devices: 25.7 us -> 20.1 us  [per_device(): lax.all_gather(moved, 'blk', axis=0, tiled=True, axis_index_groups=Y_GROUPS)]
    ppermute x1, waiting for transfers between devices: 0.01 us -> 4.36 us  [per_device(): moved = lax.ppermute(out_proj, ('blk', 'head'), PROJ_MOVE)]
    unnamed x34 -> x32, local copies, waits for them, and re-layouts: 6.24 us -> 6.34 us
  transfers between devices with their start and end apart: 21 -> 17, of which waited for: 12 -> 10; matrix products, arithmetic and copies ran while one was open for 3% -> 3% of each run, Pallas kernels for 5% -> 4%
where the time goes in v4:
time: 311 us; the launch traced here: 310 us
  waiting for transfers between devices  166 us (53%)
  starting transfers between devices  69 us (22%)
  Pallas kernels  21.1 us (7%)
  blocking collectives  19.2 us (6%)
  local copies, waits for them, and re-layouts  14 us (5%)
  between operations  13.8 us (4%)
  other arithmetic  4.18 us (1%)
    ppermute x1, waiting for transfers between devices, per_device(): down_chip = lax.ppermute(w_down[0], 'head', CHIP_SWAP)  44 us
    all_to_all x3, waiting for transfers between devices, spread_over(): lax.all_to_all(jnp.broadcast_to(x[None], (count,) + x.shape), axis, 0, 0,...  42.2 us
    all_to_all x1, waiting for transfers between devices, per_device(): lax.all_to_all(act, 'head', 0, 0, tiled=True, axis_index_groups=ACROSS)  20.1 us
    all_gather x1, waiting for transfers between devices, per_device(): lax.all_gather(moved, 'blk', axis=0, tiled=True, axis_index_groups=Y_GROUPS)  20.1 us
    all_to_all x1, blocking collectives, spread_over(): lax.all_to_all(jnp.broadcast_to(x[None], (count,) + x.shape), axis, 0, 0,...  19.2 us
    all_to_all x1, waiting for transfers between devices, per_device(): lax.all_to_all(sent, ('blk', 'head'), 0, 0, tiled=True, axis_index_groups...  19.1 us
    all_to_all x3, starting transfers between devices, spread_over(): lax.all_to_all(jnp.broadcast_to(x[None], (count,) + x.shape), axis, 0, 0,...  14.4 us
    all_to_all x1, starting transfers between devices, per_device(): lax.all_to_all(partial, ('blk', 'head'), 0, 0, tiled=True, axis_index_gro...  10.2 us
  transfers between devices with their start and end apart: 17, of which 10 were waited for; matrix products, arithmetic and copies ran while one was open for 3% of the time, Pallas kernels for 4%

profile of v4, /device:TPU:8, one launch (start us, length us, event | category | flops | bytes accessed | tf_op | source)
XLA Modules:
  0.0 309.6 jit_solution(7638686400328893316)
XLA Ops:
  7.5 19.2 %all_to_all.45 = bf16[8,32,576]{2,1,0:T(8,128)(2,1)S(1)} all-to-all(bf16[8,32,576]{2,1,0:T(8,128)(2,1)S(1)} %broadcast_in_dim.18), channel_id=1, replica_groups={{0,64,128,192,256,320,384,448},{16,80,144,208,272,336,400,464},{32,96,1..., dimensions={0} | all-to-all | bytes 589824 | tf_op jit(solution)/shard_map/all_to_all | solution.py:261
  27.9 4.3 %all-to-all-start.1 = ((bf16[4,576,256]{2,1,0:T(8,128)(2,1)}), bf16[4,576,256]{2,1,0:T(8,128)(2,1)S(1)}, u32[]{:S(2)}, u32[]{:S(2)}) async-start(bf16[4,576,256]{2,1,0:T(8,128)(2,1)} %broadcast_in_dim.19), calls=%async_computation.1 | async-start | bytes 2359296 | tf_op jit(solution)/shard_map/all_to_all | solution.py:261
  34.1 4.4 %collective-permute-done.1 = bf16[512,128]{1,0:T(8,128)(2,1)S(1)} collective-permute-done((bf16[512,128]{1,0:T(8,128)(2,1)S(1)}, bf16[512,128]{1,0:T(8,128)(2,1)S(1)}, u32[]{:S(2)}, u32[]{:S(2)}) %collective-permute-start.1) | collective-permute-done | bytes 131104 | tf_op jit(solution)/shard_map/ppermute | solution.py:277
  39.1 7.0 %all-to-all-done.1.own_ref = bf16[4,576,256]{2,1,0:T(8,128)(2,1)S(1)} async-done(((bf16[4,576,256]{2,1,0:T(8,128)(2,1)}), bf16[4,576,256]{2,1,0:T(8,128)(2,1)S(1)}, u32[]{:S(2)}, u32[]{:S(2)}) %all-to-all-start.1) | async-done | bytes 1179680 | tf_op jit(solution)/shard_map/all_to_all | solution.py:261
  51.9 5.0 %attend.1 = bf16[8,64,512]{2,1,0:T(8,128)(2,1)} custom-call(s32[3]{0:T(128)} %pad_add_fusion.place_ref, bf16[64,2304]{1,0:T(8,128)(2,1)} %q_ref.1, bf16[4,576,256]{2,1,0:T(8,128)(2,1)} %copy-done.3, bf16[4,576,256]{2,1,0:T(8,128)(2,1)} %copy-done.7, bf16[4,512,128]{2,1,0:T(8,128)(2,1)} %lift_ref.1), custom_call_target="tpu_custom_call" | custom-call | tf_op jit(solution)/shard_map/attend/pallas_call | solution.py:192
  56.8 3.6 %all-to-all-start.2 = ((bf16[8,64,512]{2,1,0:T(8,128)(2,1)}), bf16[8,64,512]{2,1,0:T(8,128)(2,1)S(1)}, u32[]{:S(2)}, u32[]{:S(2)}) async-start(bf16[8,64,512]{2,1,0:T(8,128)(2,1)} %attend.1), calls=%async_computation.2 | async-start | bytes 1048576 | tf_op jit(solution)/shard_map/all_to_all | solution.py:296
  60.5 20.1 %all-gather.2.cloned.1.call-done = bf16[4096,128]{1,0:T(8,128)(2,1)} async-done(((bf16[512,128]{1,0:T(8,128)(2,1)}), bf16[4096,128]{1,0:T(8,128)(2,1)}) %all-gather.2.cloned.1.call-update) | async-done | bytes 1048592 | tf_op jit(solution)/shard_map/all_gather | solution.py:278
  81.3 2.5 project.1
  83.9 10.2 %all-to-all-start.3 = ((bf16[32,32,128]{2,1,0:T(8,128)(2,1)}), bf16[32,32,128]{2,1,0:T(8,128)(2,1)S(1)}, u32[]{:S(2)}, u32[]{:S(2)}) async-start(bf16[32,32,128]{2,1,0:T(8,128)(2,1)} %project.1), calls=%async_computation.3 | async-start | bytes 524288 | tf_op jit(solution)/shard_map/all_to_all | solution.py:300
  95.6 3.7 %collective-permute-start.3 = (bf16[4096,256]{1,0:T(8,128)(2,1)S(1)}, bf16[4096,256]{1,0:T(8,128)(2,1)}, u32[]{:S(2)}, u32[]{:S(2)}) collective-permute-start(bf16[4096,256]{1,0:T(8,128)(2,1)S(1)} %pad_maximum_fusion.refs_0_), channel_id=1, source_target_pairs={{0,2},{1,3},{2,0},{3,1},{4,6},{5,7},{6,4},{7,5},{8,10},{9,11},{10,... | collective-permute-start | bytes 6291464 | tf_op jit(solution)/shard_map/ppermute | solution.py:285
  99.5 6.7 %all-to-all-done.3 = bf16[32,32,128]{2,1,0:T(8,128)(2,1)S(1)} async-done(((bf16[32,32,128]{2,1,0:T(8,128)(2,1)}), bf16[32,32,128]{2,1,0:T(8,128)(2,1)S(1)}, u32[]{:S(2)}, u32[]{:S(2)}) %all-to-all-start.3) | async-done | bytes 262176 | tf_op jit(solution)/shard_map/all_to_all | solution.py:300
  107.2 3.5 %all-to-all-start.4 = ((f32[4,8,32,128]{3,2,1,0:T(8,128)}), f32[4,8,32,128]{3,2,1,0:T(8,128)S(1)}, u32[]{:S(2)}, u32[]{:S(2)}) async-start(f32[4,8,32,128]{3,2,1,0:T(8,128)} %broadcast_in_dim.20), calls=%async_computation.4 | async-start | bytes 1048576 | tf_op jit(solution)/shard_map/all_to_all | solution.py:261
  112.9 35.2 %all-to-all-done.4.shared_ref = f32[4,8,32,128]{3,2,1,0:T(8,128)S(1)} async-done(((f32[4,8,32,128]{3,2,1,0:T(8,128)}), f32[4,8,32,128]{3,2,1,0:T(8,128)S(1)}, u32[]{:S(2)}, u32[]{:S(2)}) %all-to-all-start.4) | async-done | bytes 524320 | tf_op jit(solution)/shard_map/all_to_all | solution.py:261
  152.7 8.1 %all-to-all-start.5 = ((bf16[32,40,128]{2,1,0:T(8,128)(2,1)}), bf16[32,40,128]{2,1,0:T(8,128)(2,1)S(1)}, u32[]{:S(2)}, u32[]{:S(2)}) async-start(bf16[32,40,128]{2,1,0:T(8,128)(2,1)} %reshape.103), calls=%async_computation.5 | async-start | bytes 655360 | tf_op jit(solution)/shard_map/all_to_all | solution.py:336
  165.2 7.6 %all-to-all-done.5 = bf16[32,40,128]{2,1,0:T(8,128)(2,1)S(1)} async-done(((bf16[32,40,128]{2,1,0:T(8,128)(2,1)}), bf16[32,40,128]{2,1,0:T(8,128)(2,1)S(1)}, u32[]{:S(2)}, u32[]{:S(2)}) %all-to-all-start.5) | async-done | bytes 327712 | tf_op jit(solution)/shard_map/all_to_all | solution.py:336
  174.3 6.6 %all-to-all-start.6 = ((bf16[4,160,1024]{2,1,0:T(8,128)(2,1)}), bf16[4,160,1024]{2,1,0:T(8,128)(2,1)S(1)}, u32[]{:S(2)}, u32[]{:S(2)}) async-start(bf16[4,160,1024]{2,1,0:T(8,128)(2,1)} %broadcast_in_dim.48), calls=%async_computation.6 | async-start | bytes 2621440 | tf_op jit(solution)/shard_map/all_to_all | solution.py:261
  180.9 2.5 collective-permute-start.6
  185.3 44.0 %collective-permute-done.6.refs_2_ = bf16[2048,256]{1,0:T(8,128)(2,1)} collective-permute-done((bf16[2048,256]{1,0:T(8,128)(2,1)}, bf16[2048,256]{1,0:T(8,128)(2,1)}, u32[]{:S(2)}, u32[]{:S(2)}) %collective-permute-start.6) | collective-permute-done | bytes 1048608 | tf_op jit(solution)/shard_map/ppermute | solution.py:286
  232.3 6.7 %hidden.1 = bf16[4,160,512]{2,1,0:T(8,128)(2,1)} custom-call(s32[3]{0:T(128)} %pad_add_fusion.place_ref, bf16[4,160,1024]{2,1,0:T(8,128)(2,1)} %copy-done.2, bf16[4096,256]{1,0:T(8,128)(2,1)} %copy-done.1, bf16[4096,256]{1,0:T(8,128)(2,1)} %collective-permute-done.2.refs_1_, bf16[4096,256]{1,0:T(8,128)(2,1)} %collective-permute-done.3.refs_2_, ...), custom_call_target="tpu_custom_call" | custom-call | tf_op jit(solution)/shard_map/hidden/pallas_call | solution.py:230
  239.1 6.9 %all-to-all-start.7 = ((bf16[4,160,512]{2,1,0:T(8,128)(2,1)}), bf16[4,160,512]{2,1,0:T(8,128)(2,1)S(1)}, u32[]{:S(2)}, u32[]{:S(2)}) async-start(bf16[4,160,512]{2,1,0:T(8,128)(2,1)} %hidden.1), calls=%async_computation.7 | async-start | bytes 1310720 | tf_op jit(solution)/shard_map/all_to_all | solution.py:340
  245.9 20.1 %all-to-all-done.7.act_ref = bf16[4,160,512]{2,1,0:T(8,128)(2,1)S(1)} async-done(((bf16[4,160,512]{2,1,0:T(8,128)(2,1)}), bf16[4,160,512]{2,1,0:T(8,128)(2,1)S(1)}, u32[]{:S(2)}, u32[]{:S(2)}) %all-to-all-start.7) | async-done | bytes 655392 | tf_op jit(solution)/shard_map/all_to_all | solution.py:340
  266.9 5.1 %down.1 = bf16[160,1024]{1,0:T(8,128)(2,1)} custom-call(s32[3]{0:T(128)} %pad_add_fusion.place_ref, bf16[4,160,512]{2,1,0:T(8,128)(2,1)} %copy-done.4, bf16[2048,256]{1,0:T(8,128)(2,1)} %bitcast.52, bf16[2048,256]{1,0:T(8,128)(2,1)} %collective-permute-done.5.refs_1_, bf16[2048,256]{1,0:T(8,128)(2,1)} %collective-permute-done.6.refs_2_, ...), custom_call_target="tpu_custom_call" | custom-call | tf_op jit(solution)/shard_map/down/pallas_call | solution.py:249
  274.3 7.7 %all-to-all-start.8 = ((bf16[128,10,128]{2,1,0:T(8,128)(2,1)}), bf16[128,10,128]{2,1,0:T(8,128)(2,1)S(1)}, u32[]{:S(2)}, u32[]{:S(2)}) async-start(bf16[128,10,128]{2,1,0:T(8,128)(2,1)} %reshape.105), calls=%async_computation.8 | async-start | bytes 1048576 | tf_op jit(solution)/shard_map/all_to_all | solution.py:347
  282.6 19.1 %all-to-all-done.8 = bf16[128,10,128]{2,1,0:T(8,128)(2,1)S(1)} async-done(((bf16[128,10,128]{2,1,0:T(8,128)(2,1)}), bf16[128,10,128]{2,1,0:T(8,128)(2,1)S(1)}, u32[]{:S(2)}, u32[]{:S(2)}) %all-to-all-start.8) | async-done | bytes 327712 | tf_op jit(solution)/shard_map/all_to_all | solution.py:347
  (85 shorter events, 36.2 us)
Async XLA Ops:
  26.6 5.6 %copy-start.14 = (bf16[512,128]{1,0:T(8,128)(2,1)S(1)}, bf16[512,128]{1,0:T(8,128)(2,1)}, u32[]{:S(2)}) copy-start(bf16[512,128]{1,0:T(8,128)(2,1)} %param.14) | copy-start | bytes 393220
  27.9 18.2 %all-to-all-start.1 = ((bf16[4,576,256]{2,1,0:T(8,128)(2,1)}), bf16[4,576,256]{2,1,0:T(8,128)(2,1)S(1)}, u32[]{:S(2)}, u32[]{:S(2)}) async-start(bf16[4,576,256]{2,1,0:T(8,128)(2,1)} %broadcast_in_dim.19), calls=%async_computation.1 | async-start | bytes 2359296 | tf_op jit(solution)/shard_map/all_to_all | solution.py:261
  32.2 48.3 %all-gather.2.cloned.1.call-start = ((), (), s32[]{:S(2)}) async-start(), calls=%async_computation.9 | async-start | bytes 1179648 | tf_op jit(solution)/shard_map/all_gather | solution.py:278
  32.2 6.3 %collective-permute-start.1 = (bf16[512,128]{1,0:T(8,128)(2,1)S(1)}, bf16[512,128]{1,0:T(8,128)(2,1)S(1)}, u32[]{:S(2)}, u32[]{:S(2)}) collective-permute-start(bf16[512,128]{1,0:T(8,128)(2,1)S(1)} %copy-done.14), channel_id=1, source_target_pairs={{0,0},{1,64},{2,2},{3,66},{4,4},{5,68},{6,6},{7,70},{8,8},{9,72},{... | collective-permute-start | bytes 393224 | tf_op jit(solution)/shard_map/ppermute | solution.py:277
  46.1 4.7 %collective-permute-start = (bf16[4,576,256]{2,1,0:T(8,128)(2,1)S(1)}, bf16[4,576,256]{2,1,0:T(8,128)(2,1)S(1)}, u32[]{:S(2)}, u32[]{:S(2)}) collective-permute-start(bf16[4,576,256]{2,1,0:T(8,128)(2,1)S(1)} %all-to-all-done.1.own_ref), channel_id=1, source_target_pairs={{0,1},{1,0},{2,3},{3,2},{4,5},{5,4},{6,7},{7,6},{8,9},{9,8},{10,11... | collective-permute-start | bytes 3538952 | tf_op jit(solution)/shard_map/ppermute | solution.py:291
  56.8 37.2 %copy-start.8 = (bf16[1,4096,128]{2,1,0:T(8,128)(2,1)S(1)}, bf16[1,4096,128]{2,1,0:T(8,128)(2,1)}, u32[]{:S(2)}) copy-start(bf16[1,4096,128]{2,1,0:T(8,128)(2,1)} %param.18) | copy-start | bytes 3145732
  56.8 23.7 %all-to-all-start.2 = ((bf16[8,64,512]{2,1,0:T(8,128)(2,1)}), bf16[8,64,512]{2,1,0:T(8,128)(2,1)S(1)}, u32[]{:S(2)}, u32[]{:S(2)}) async-start(bf16[8,64,512]{2,1,0:T(8,128)(2,1)} %attend.1), calls=%async_computation.2 | async-start | bytes 1048576 | tf_op jit(solution)/shard_map/all_to_all | solution.py:296
  83.9 22.4 %all-to-all-start.3 = ((bf16[32,32,128]{2,1,0:T(8,128)(2,1)}), bf16[32,32,128]{2,1,0:T(8,128)(2,1)S(1)}, u32[]{:S(2)}, u32[]{:S(2)}) async-start(bf16[32,32,128]{2,1,0:T(8,128)(2,1)} %project.1), calls=%async_computation.3 | async-start | bytes 524288 | tf_op jit(solution)/shard_map/all_to_all | solution.py:300
  94.1 5.2 %copy-start.11 = (bf16[64,256]{1,0:T(8,128)(2,1)S(1)}, bf16[64,256]{1,0:T(8,128)(2,1)}, u32[]{:S(2)}) copy-start(bf16[64,256]{1,0:T(8,128)(2,1)} %param.10) | copy-start | bytes 98308
  94.1 5.2 %copy-start.12 = (s32[64,8]{0,1:T(8,128)S(1)}, s32[64,8]{0,1:T(8,128)}, u32[]{:S(2)}) copy-start(s32[64,8]{0,1:T(8,128)} %param.15) | copy-start | bytes 6148
  95.6 65.3 %copy-start.1 = (bf16[4096,256]{1,0:T(8,128)(2,1)}, bf16[4096,256]{1,0:T(8,128)(2,1)S(1)}, u32[]{:S(2)}) copy-start(bf16[4096,256]{1,0:T(8,128)(2,1)S(1)} %pad_maximum_fusion.refs_0_) | copy-start | bytes 6291460
  95.6 67.2 %collective-permute-start.3 = (bf16[4096,256]{1,0:T(8,128)(2,1)S(1)}, bf16[4096,256]{1,0:T(8,128)(2,1)}, u32[]{:S(2)}, u32[]{:S(2)}) collective-permute-start(bf16[4096,256]{1,0:T(8,128)(2,1)S(1)} %pad_maximum_fusion.refs_0_), channel_id=1, source_target_pairs={{0,2},{1,3},{2,0},{3,1},{4,6},{5,7},{6,4},{7,5},{8,10},{9,11},{10,... | collective-permute-start | bytes 6291464 | tf_op jit(solution)/shard_map/ppermute | solution.py:285
  107.2 40.9 %all-to-all-start.4 = ((f32[4,8,32,128]{3,2,1,0:T(8,128)}), f32[4,8,32,128]{3,2,1,0:T(8,128)S(1)}, u32[]{:S(2)}, u32[]{:S(2)}) async-start(f32[4,8,32,128]{3,2,1,0:T(8,128)} %broadcast_in_dim.20), calls=%async_computation.4 | async-start | bytes 1048576 | tf_op jit(solution)/shard_map/all_to_all | solution.py:261
  152.7 20.1 %all-to-all-start.5 = ((bf16[32,40,128]{2,1,0:T(8,128)(2,1)}), bf16[32,40,128]{2,1,0:T(8,128)(2,1)S(1)}, u32[]{:S(2)}, u32[]{:S(2)}) async-start(bf16[32,40,128]{2,1,0:T(8,128)(2,1)} %reshape.103), calls=%async_computation.5 | async-start | bytes 655360 | tf_op jit(solution)/shard_map/all_to_all | solution.py:336
  160.8 70.4 %collective-permute-start.2 = (bf16[4096,256]{1,0:T(8,128)(2,1)S(1)}, bf16[4096,256]{1,0:T(8,128)(2,1)}, u32[]{:S(2)}, u32[]{:S(2)}) collective-permute-start(bf16[4096,256]{1,0:T(8,128)(2,1)S(1)} %pad_maximum_fusion.refs_0_), channel_id=1, source_target_pairs={{0,1},{1,0},{2,3},{3,2},{4,5},{5,4},{6,7},{7,6},{8,9},{9,8},{10,11... | collective-permute-start | bytes 6291464 | tf_op jit(solution)/shard_map/ppermute | solution.py:267
  162.8 68.4 %collective-permute-start.4 = (bf16[4096,256]{1,0:T(8,128)(2,1)}, bf16[4096,256]{1,0:T(8,128)(2,1)}, u32[]{:S(2)}, u32[]{:S(2)}) collective-permute-start(bf16[4096,256]{1,0:T(8,128)(2,1)} %collective-permute-done.3.refs_2_), channel_id=1, source_target_pairs={{0,1},{1,0},{2,3},{3,2},{4,5},{5,4},{6,7},{7,6},{8,9},{9,8},{10,11... | collective-permute-start | bytes 6291464 | tf_op jit(solution)/shard_map/ppermute | solution.py:268
  174.3 57.0 %all-to-all-start.6 = ((bf16[4,160,1024]{2,1,0:T(8,128)(2,1)}), bf16[4,160,1024]{2,1,0:T(8,128)(2,1)S(1)}, u32[]{:S(2)}, u32[]{:S(2)}) async-start(bf16[4,160,1024]{2,1,0:T(8,128)(2,1)} %broadcast_in_dim.48), calls=%async_computation.6 | async-start | bytes 2621440 | tf_op jit(solution)/shard_map/all_to_all | solution.py:261
  180.9 48.4 %collective-permute-start.6 = (bf16[2048,256]{1,0:T(8,128)(2,1)}, bf16[2048,256]{1,0:T(8,128)(2,1)}, u32[]{:S(2)}, u32[]{:S(2)}) collective-permute-start(bf16[2048,256]{1,0:T(8,128)(2,1)} %bitcast.50), channel_id=1, source_target_pairs={{0,2},{1,3},{2,0},{3,1},{4,6},{5,7},{6,4},{7,5},{8,10},{9,11},{10,... | collective-permute-start | bytes 3145736 | tf_op jit(solution)/shard_map/ppermute | solution.py:286
  183.4 62.5 %collective-permute-start.5 = (bf16[2048,256]{1,0:T(8,128)(2,1)}, bf16[2048,256]{1,0:T(8,128)(2,1)}, u32[]{:S(2)}, u32[]{:S(2)}) collective-permute-start(bf16[2048,256]{1,0:T(8,128)(2,1)} %bitcast.51), channel_id=1, source_target_pairs={{0,1},{1,0},{2,3},{3,2},{4,5},{5,4},{6,7},{7,6},{8,9},{9,8},{10,11... | collective-permute-start | bytes 3145736 | tf_op jit(solution)/shard_map/ppermute | solution.py:267
  229.3 16.7 %collective-permute-start.7 = (bf16[2048,256]{1,0:T(8,128)(2,1)}, bf16[2048,256]{1,0:T(8,128)(2,1)}, u32[]{:S(2)}, u32[]{:S(2)}) collective-permute-start(bf16[2048,256]{1,0:T(8,128)(2,1)} %collective-permute-done.6.refs_2_), channel_id=1, source_target_pairs={{0,1},{1,0},{2,3},{3,2},{4,5},{5,4},{6,7},{7,6},{8,9},{9,8},{10,11... | collective-permute-start | bytes 3145736 | tf_op jit(solution)/shard_map/ppermute | solution.py:268
  239.1 27.0 %all-to-all-start.7 = ((bf16[4,160,512]{2,1,0:T(8,128)(2,1)}), bf16[4,160,512]{2,1,0:T(8,128)(2,1)S(1)}, u32[]{:S(2)}, u32[]{:S(2)}) async-start(bf16[4,160,512]{2,1,0:T(8,128)(2,1)} %hidden.1), calls=%async_computation.7 | async-start | bytes 1310720 | tf_op jit(solution)/shard_map/all_to_all | solution.py:340
  272.0 10.0 %copy-start.13 = (f32[64,8]{0,1:T(8,128)S(1)}, f32[64,8]{0,1:T(8,128)}, u32[]{:S(2)}) copy-start(f32[64,8]{0,1:T(8,128)} %param.16) | copy-start | bytes 6148
  273.2 28.6 %copy-start.10 = (bf16[64,256]{1,0:T(8,128)(2,1)S(1)}, bf16[64,256]{1,0:T(8,128)(2,1)}, u32[]{:S(2)}) copy-start(bf16[64,256]{1,0:T(8,128)(2,1)} %get-tuple-element.7) | copy-start | bytes 98308
  274.3 27.3 %all-to-all-start.8 = ((bf16[128,10,128]{2,1,0:T(8,128)(2,1)}), bf16[128,10,128]{2,1,0:T(8,128)(2,1)S(1)}, u32[]{:S(2)}, u32[]{:S(2)}) async-start(bf16[128,10,128]{2,1,0:T(8,128)(2,1)} %reshape.105), calls=%async_computation.8 | async-start | bytes 1048576 | tf_op jit(solution)/shard_map/all_to_all | solution.py:347
  (8 other events, 10.9 us)
Sparse Core Ops, SparseCore 0:
  39.3 41.2 all-gather.1

commit v5 on v4

--- a/solution.py
+++ b/solution.py
@@ -90,7 +90,7 @@
     total = 0.0
     context = 0.0
     for (ref, x, offset), raw in zip(chunks, scores):
-        weights = jnp.where(room >= offset, jnp.exp(raw - row_max), 0.0)
+        weights = jnp.exp(raw - row_max)
         total = total + weights
         context = context + lax.dot_general(
             weights.astype(jnp.bfloat16),
@@ -125,7 +125,7 @@
                     ]
 
 
-def mid_kernel(place_ref, shared_ref, quad_ref, own_ref):
+def mid_kernel(place_ref, shared_ref, select_ref, out_ref, own_ref):
     for i in range(QUAD):
         parts = []
         for p in range(2):
@@ -135,7 +135,9 @@
             ]
             parts.append(jnp.concatenate(wide, axis=1))
         mid = jnp.concatenate(parts, axis=0).astype(jnp.bfloat16)
-        quad_ref[:, i * 256 : (i + 1) * 256] = mid
+        out_ref[:, i * 256 : (i + 1) * 256] = jnp.dot(
+            select_ref[...], mid, preferred_element_type=jnp.float32
+        ).astype(jnp.bfloat16)
 
         @pl.when(place_ref[2] == i)
         def _():
@@ -151,7 +153,7 @@
         acc_ref[...] = jnp.zeros_like(acc_ref)
         square_ref[...] = jnp.zeros_like(square_ref)
 
-    rows = rows_ref[step]
+    rows = rows_ref[0]
     for j in range(QUAD):
         acc_ref[j] += jnp.dot(rows, weight_refs[j][...], preferred_element_type=jnp.float32)
     wide = rows.astype(jnp.float32)
@@ -174,18 +176,24 @@
 
 
 def down_kernel(place_ref, act_ref, *refs):
-    weight_refs, out_ref = refs[:QUAD], refs[QUAD]
-    wide = jnp.concatenate([act_ref[i] for i in range(QUAD)], axis=1)
+    weight_refs, (out_ref, acc_ref) = refs[:QUAD], refs[QUAD:]
+    step = pl.program_id(0)
+
+    @pl.when(step == 0)
+    def _():
+        acc_ref[...] = jnp.zeros_like(acc_ref)
+
+    act = act_ref[0]
     for j in range(QUAD):
-        owner = jnp.bitwise_xor(place_ref[2], j)
-        result = jnp.dot(wide, weight_refs[j][...], preferred_element_type=jnp.float32).astype(
-            jnp.bfloat16
-        )
-        for other in range(QUAD):
-
-            @pl.when(owner == other)
-            def _():
-                out_ref[:, other * 256 : (other + 1) * 256] = result
+        acc_ref[j] += jnp.dot(act, weight_refs[j][...], preferred_element_type=jnp.float32)
+
+    @pl.when(step == QUAD - 1)
+    def _():
+        for j in range(QUAD):
+            owner = jnp.bitwise_xor(place_ref[2], j)
+            result = acc_ref[j].astype(jnp.bfloat16).astype(jnp.float32)
+            for b in range(N_BLK):
+                out_ref[b * QUAD + owner] = result[b * PART : (b + 1) * PART].astype(jnp.bfloat16)
 
 
 def attend(place, queries, own, other, value_up):
@@ -209,20 +217,18 @@
     )(lifted, proj)
 
 
-def middle(place, shared):
+def middle(place, shared, select):
     return pl.pallas_call(
         mid_kernel,
         out_shape=(
-            jax.ShapeDtypeStruct((TOK, QUAD * 256), jnp.bfloat16),
+            jax.ShapeDtypeStruct((ROWS, QUAD * 256), jnp.bfloat16),
             jax.ShapeDtypeStruct((TOK, 256), jnp.bfloat16),
         ),
-        in_specs=[
-            pl.BlockSpec(memory_space=pltpu.SMEM),
-            pl.BlockSpec(memory_space=pltpu.VMEM),
-        ],
+        in_specs=[pl.BlockSpec(memory_space=pltpu.SMEM)]
+        + [pl.BlockSpec(memory_space=pltpu.VMEM)] * 2,
         out_specs=(pl.BlockSpec(memory_space=pltpu.VMEM),) * 2,
         name="middle",
-    )(place, shared)
+    )(place, shared, select)
 
 
 def hidden(place, rows, weights):
@@ -233,7 +239,7 @@
         grid=(QUAD,),
         in_specs=[
             pl.BlockSpec(memory_space=pltpu.SMEM),
-            pl.BlockSpec(memory_space=pltpu.VMEM),
+            pl.BlockSpec((1, ROWS, depth), lambda i: (i, 0, 0)),
         ]
         + [pl.BlockSpec((depth, 256), lambda i: (i, 0))] * QUAD,
         out_specs=pl.BlockSpec((QUAD, ROWS, QUAD * 128), lambda i: (0, 0, 0)),
@@ -246,12 +252,18 @@
 
 
 def down(place, act, weights):
+    depth = QUAD * 128
     return pl.pallas_call(
         down_kernel,
-        out_shape=jax.ShapeDtypeStruct((ROWS, QUAD * 256), jnp.bfloat16),
-        in_specs=[pl.BlockSpec(memory_space=pltpu.SMEM)]
-        + [pl.BlockSpec(memory_space=pltpu.VMEM)] * (1 + QUAD),
-        out_specs=pl.BlockSpec(memory_space=pltpu.VMEM),
+        out_shape=jax.ShapeDtypeStruct((N_BLK * QUAD, PART, 256), jnp.bfloat16),
+        grid=(QUAD,),
+        in_specs=[
+            pl.BlockSpec(memory_space=pltpu.SMEM),
+            pl.BlockSpec((1, ROWS, depth), lambda i: (i, 0, 0)),
+        ]
+        + [pl.BlockSpec((depth, 256), lambda i: (i, 0))] * QUAD,
+        out_specs=pl.BlockSpec((N_BLK * QUAD, PART, 256), lambda i: (0, 0, 0)),
+        scratch_shapes=[pltpu.VMEM((QUAD, ROWS, 256), jnp.float32)],
         name="down",
     )(place, act, *weights)
 
@@ -302,9 +314,6 @@
     token_blocks = jnp.stack([tokens[:, :128], tokens[:, 128:]]).reshape(4, HALF, 128)
     shared = jnp.concatenate([summed, token_blocks.astype(jnp.float32)], axis=0)
     shared = spread_over(shared, "head", QUADS).reshape(QUAD, 8, HALF, 128)
-    mid_quad, mid_state = middle(place, shared)
-    mid_wide = mid_state.astype(jnp.float32)
-
     row_count = tokens.shape[0]
     flat_ids = expert_ids.reshape(-1)
     choose_count = expert_ids.shape[1]
@@ -328,22 +337,15 @@
         axis=2,
     )
 
-    outgoing = (
-        jnp.dot(select, mid_quad, preferred_element_type=jnp.float32)
-        .astype(jnp.bfloat16)
-        .reshape(N_BLK, PART * QUAD * 2, 128)
-    )
+    chosen, mid_state = middle(place, shared, select)
+    mid_wide = mid_state.astype(jnp.float32)
+    outgoing = chosen.reshape(N_BLK, PART * QUAD * 2, 128)
     incoming = lax.all_to_all(outgoing, "blk", 0, 0, tiled=True)
     rows_here = incoming.reshape(ROWS, QUAD * 256)
     rows = spread_over(rows_here, "head", ACROSS).reshape(QUAD, ROWS, QUAD * 256)
     act = hidden(place, rows, gate_up_quad)
     acts = lax.all_to_all(act, "head", 0, 0, tiled=True, axis_index_groups=ACROSS)
-    expert_out = down(place, acts, down_quad)
-    sent = (
-        expert_out.reshape(N_BLK, PART, QUAD, 256)
-        .transpose(0, 2, 1, 3)
-        .reshape(N_BLK * QUAD, PART * 2, 128)
-    )
+    sent = down(place, acts, down_quad)
     returned = lax.all_to_all(
         sent, ("blk", "head"), 0, 0, tiled=True, axis_index_groups=BLK_QUAD
     )

time: 311 us -> 308 us (level)
  no operation moved by 1% of the time
where the time goes in v5:
time: 308 us; the launch traced here: 307 us
  waiting for transfers between devices  166 us (54%)
  starting transfers between devices  69.2 us (22%)
  Pallas kernels  20.9 us (7%)
  blocking collectives  19.2 us (6%)
  between operations  13.7 us (4%)
  local copies, waits for them, and re-layouts  13.3 us (4%)
  other arithmetic  4.18 us (1%)
    ppermute x1, waiting for transfers between devices, per_device(): down_chip = lax.ppermute(w_down[0], 'head', CHIP_SWAP)  44 us
    all_to_all x3, waiting for transfers between devices, spread_over(): lax.all_to_all(jnp.broadcast_to(x[None], (count,) + x.shape), axis, 0, 0,...  41.5 us
    all_gather x1, waiting for transfers between devices, per_device(): lax.all_gather(moved, 'blk', axis=0, tiled=True, axis_index_groups=Y_GROUPS)  20.2 us
    all_to_all x1, waiting for transfers between devices, per_device(): lax.all_to_all(act, 'head', 0, 0, tiled=True, axis_index_groups=ACROSS)  20.1 us
    all_to_all x1, blocking collectives, spread_over(): lax.all_to_all(jnp.broadcast_to(x[None], (count,) + x.shape), axis, 0, 0,...  19.2 us
    all_to_all x1, waiting for transfers between devices, per_device(): lax.all_to_all(sent, ('blk', 'head'), 0, 0, tiled=True, axis_index_groups...  19.1 us
    all_to_all x3, starting transfers between devices, spread_over(): lax.all_to_all(jnp.broadcast_to(x[None], (count,) + x.shape), axis, 0, 0,...  14.4 us
    all_to_all x1, starting transfers between devices, per_device(): lax.all_to_all(partial, ('blk', 'head'), 0, 0, tiled=True, axis_index_gro...  10.2 us
  transfers between devices with their start and end apart: 17, of which 10 were waited for; matrix products, arithmetic and copies ran while one was open for 3% of the time, Pallas kernels for 4%

profile of v5, /device:TPU:8, one launch (start us, length us, event | category | flops | bytes accessed | tf_op | source)
XLA Modules:
  0.0 307.2 jit_solution(2375797250011626576)
XLA Ops:
  7.5 19.2 %all_to_all.45 = bf16[8,32,576]{2,1,0:T(8,128)(2,1)S(1)} all-to-all(bf16[8,32,576]{2,1,0:T(8,128)(2,1)S(1)} %broadcast_in_dim.18), channel_id=1, replica_groups={{0,64,128,192,256,320,384,448},{16,80,144,208,272,336,400,464},{32,96,1..., dimensions={0} | all-to-all | bytes 589824 | tf_op jit(solution)/shard_map/all_to_all | solution.py:273
  27.9 4.3 %all-to-all-start.1 = ((bf16[4,576,256]{2,1,0:T(8,128)(2,1)}), bf16[4,576,256]{2,1,0:T(8,128)(2,1)S(1)}, u32[]{:S(2)}, u32[]{:S(2)}) async-start(bf16[4,576,256]{2,1,0:T(8,128)(2,1)} %broadcast_in_dim.19), calls=%async_computation.1 | async-start | bytes 2359296 | tf_op jit(solution)/shard_map/all_to_all | solution.py:273
  34.1 4.4 %collective-permute-done.1 = bf16[512,128]{1,0:T(8,128)(2,1)S(1)} collective-permute-done((bf16[512,128]{1,0:T(8,128)(2,1)S(1)}, bf16[512,128]{1,0:T(8,128)(2,1)S(1)}, u32[]{:S(2)}, u32[]{:S(2)}) %collective-permute-start.1) | collective-permute-done | bytes 131104 | tf_op jit(solution)/shard_map/ppermute | solution.py:289
  39.1 7.0 %all-to-all-done.1.own_ref = bf16[4,576,256]{2,1,0:T(8,128)(2,1)S(1)} async-done(((bf16[4,576,256]{2,1,0:T(8,128)(2,1)}), bf16[4,576,256]{2,1,0:T(8,128)(2,1)S(1)}, u32[]{:S(2)}, u32[]{:S(2)}) %all-to-all-start.1) | async-done | bytes 1179680 | tf_op jit(solution)/shard_map/all_to_all | solution.py:273
  51.9 4.8 %attend.1 = bf16[8,64,512]{2,1,0:T(8,128)(2,1)} custom-call(s32[3]{0:T(128)} %pad_add_fusion.place_ref, bf16[64,2304]{1,0:T(8,128)(2,1)} %q_ref.1, bf16[4,576,256]{2,1,0:T(8,128)(2,1)} %copy-done.3, bf16[4,576,256]{2,1,0:T(8,128)(2,1)} %copy-done.7, bf16[4,512,128]{2,1,0:T(8,128)(2,1)} %lift_ref.1), custom_call_target="tpu_custom_call" | custom-call | tf_op jit(solution)/shard_map/attend/pallas_call | solution.py:200
  56.7 3.6 %all-to-all-start.2 = ((bf16[8,64,512]{2,1,0:T(8,128)(2,1)}), bf16[8,64,512]{2,1,0:T(8,128)(2,1)S(1)}, u32[]{:S(2)}, u32[]{:S(2)}) async-start(bf16[8,64,512]{2,1,0:T(8,128)(2,1)} %attend.1), calls=%async_computation.2 | async-start | bytes 1048576 | tf_op jit(solution)/shard_map/all_to_all | solution.py:308
  60.3 20.2 %all-gather.2.cloned.1.call-done = bf16[4096,128]{1,0:T(8,128)(2,1)} async-done(((bf16[512,128]{1,0:T(8,128)(2,1)}), bf16[4096,128]{1,0:T(8,128)(2,1)}) %all-gather.2.cloned.1.call-update) | async-done | bytes 1048592 | tf_op jit(solution)/shard_map/all_gather | solution.py:290
  81.4 2.5 project.1
  83.9 10.2 %all-to-all-start.3 = ((bf16[32,32,128]{2,1,0:T(8,128)(2,1)}), bf16[32,32,128]{2,1,0:T(8,128)(2,1)S(1)}, u32[]{:S(2)}, u32[]{:S(2)}) async-start(bf16[32,32,128]{2,1,0:T(8,128)(2,1)} %project.1), calls=%async_computation.3 | async-start | bytes 524288 | tf_op jit(solution)/shard_map/all_to_all | solution.py:312
  95.6 3.7 %collective-permute-start.3 = (bf16[4096,256]{1,0:T(8,128)(2,1)S(1)}, bf16[4096,256]{1,0:T(8,128)(2,1)}, u32[]{:S(2)}, u32[]{:S(2)}) collective-permute-start(bf16[4096,256]{1,0:T(8,128)(2,1)S(1)} %pad_maximum_fusion.refs_0_), channel_id=1, source_target_pairs={{0,2},{1,3},{2,0},{3,1},{4,6},{5,7},{6,4},{7,5},{8,10},{9,11},{10,... | collective-permute-start | bytes 6291464 | tf_op jit(solution)/shard_map/ppermute | solution.py:297
  99.5 6.7 %all-to-all-done.3 = bf16[32,32,128]{2,1,0:T(8,128)(2,1)S(1)} async-done(((bf16[32,32,128]{2,1,0:T(8,128)(2,1)}), bf16[32,32,128]{2,1,0:T(8,128)(2,1)S(1)}, u32[]{:S(2)}, u32[]{:S(2)}) %all-to-all-start.3) | async-done | bytes 262176 | tf_op jit(solution)/shard_map/all_to_all | solution.py:312
  107.2 3.5 %all-to-all-start.4 = ((f32[4,8,32,128]{3,2,1,0:T(8,128)}), f32[4,8,32,128]{3,2,1,0:T(8,128)S(1)}, u32[]{:S(2)}, u32[]{:S(2)}) async-start(f32[4,8,32,128]{3,2,1,0:T(8,128)} %broadcast_in_dim.20), calls=%async_computation.4 | async-start | bytes 1048576 | tf_op jit(solution)/shard_map/all_to_all | solution.py:273
  113.6 34.5 %all-to-all-done.4.shared_ref = f32[4,8,32,128]{3,2,1,0:T(8,128)S(1)} async-done(((f32[4,8,32,128]{3,2,1,0:T(8,128)}), f32[4,8,32,128]{3,2,1,0:T(8,128)S(1)}, u32[]{:S(2)}, u32[]{:S(2)}) %all-to-all-start.4) | async-done | bytes 524320 | tf_op jit(solution)/shard_map/all_to_all | solution.py:273
  153.2 8.1 %all-to-all-start.5 = ((bf16[32,40,128]{2,1,0:T(8,128)(2,1)}), bf16[32,40,128]{2,1,0:T(8,128)(2,1)S(1)}, u32[]{:S(2)}, u32[]{:S(2)}) async-start(bf16[32,40,128]{2,1,0:T(8,128)(2,1)} %reshape.97), calls=%async_computation.5 | async-start | bytes 655360 | tf_op jit(solution)/shard_map/all_to_all | solution.py:343
  165.7 7.6 %all-to-all-done.5 = bf16[32,40,128]{2,1,0:T(8,128)(2,1)S(1)} async-done(((bf16[32,40,128]{2,1,0:T(8,128)(2,1)}), bf16[32,40,128]{2,1,0:T(8,128)(2,1)S(1)}, u32[]{:S(2)}, u32[]{:S(2)}) %all-to-all-start.5) | async-done | bytes 327712 | tf_op jit(solution)/shard_map/all_to_all | solution.py:343
  174.8 6.7 %all-to-all-start.6 = ((bf16[4,160,1024]{2,1,0:T(8,128)(2,1)}), bf16[4,160,1024]{2,1,0:T(8,128)(2,1)S(1)}, u32[]{:S(2)}, u32[]{:S(2)}) async-start(bf16[4,160,1024]{2,1,0:T(8,128)(2,1)} %broadcast_in_dim.48), calls=%async_computation.6 | async-start | bytes 2621440 | tf_op jit(solution)/shard_map/all_to_all | solution.py:273
  181.4 2.5 collective-permute-start.6
  185.8 44.0 %collective-permute-done.6.refs_2_ = bf16[2048,256]{1,0:T(8,128)(2,1)} collective-permute-done((bf16[2048,256]{1,0:T(8,128)(2,1)}, bf16[2048,256]{1,0:T(8,128)(2,1)}, u32[]{:S(2)}, u32[]{:S(2)}) %collective-permute-start.6) | collective-permute-done | bytes 1048608 | tf_op jit(solution)/shard_map/ppermute | solution.py:298
  232.8 6.4 %hidden.1 = bf16[4,160,512]{2,1,0:T(8,128)(2,1)} custom-call(s32[3]{0:T(128)} %pad_add_fusion.place_ref, bf16[4,160,1024]{2,1,0:T(8,128)(2,1)} %copy-done.2, bf16[4096,256]{1,0:T(8,128)(2,1)} %copy-done.1, bf16[4096,256]{1,0:T(8,128)(2,1)} %collective-permute-done.2.refs_1_, bf16[4096,256]{1,0:T(8,128)(2,1)} %collective-permute-done.3.refs_2_, ...), custom_call_target="tpu_custom_call" | custom-call | tf_op jit(solution)/shard_map/hidden/pallas_call | solution.py:236
  239.3 6.9 %all-to-all-start.7 = ((bf16[4,160,512]{2,1,0:T(8,128)(2,1)}), bf16[4,160,512]{2,1,0:T(8,128)(2,1)S(1)}, u32[]{:S(2)}, u32[]{:S(2)}) async-start(bf16[4,160,512]{2,1,0:T(8,128)(2,1)} %hidden.1), calls=%async_computation.7 | async-start | bytes 1310720 | tf_op jit(solution)/shard_map/all_to_all | solution.py:347
  246.2 20.1 %all-to-all-done.7.act_ref = bf16[4,160,512]{2,1,0:T(8,128)(2,1)S(1)} async-done(((bf16[4,160,512]{2,1,0:T(8,128)(2,1)}), bf16[4,160,512]{2,1,0:T(8,128)(2,1)S(1)}, u32[]{:S(2)}, u32[]{:S(2)}) %all-to-all-start.7) | async-done | bytes 655392 | tf_op jit(solution)/shard_map/all_to_all | solution.py:347
  267.1 4.7 %down.1 = bf16[128,5,256]{2,1,0:T(8,128)(2,1)} custom-call(s32[3]{0:T(128)} %pad_add_fusion.place_ref, bf16[4,160,512]{2,1,0:T(8,128)(2,1)} %copy-done.4, bf16[2048,256]{1,0:T(8,128)(2,1)} %bitcast.46, bf16[2048,256]{1,0:T(8,128)(2,1)} %collective-permute-done.5.refs_1_, bf16[2048,256]{1,0:T(8,128)(2,1)} %collective-permute-done.6.refs_2_, ...), custom_call_target="tpu_custom_call" | custom-call | tf_op jit(solution)/shard_map/down/pallas_call | solution.py:256
  271.8 7.8 %all-to-all-start.8 = ((bf16[128,5,256]{2,1,0:T(8,128)(2,1)}), bf16[128,5,256]{2,1,0:T(8,128)(2,1)S(1)}, u32[]{:S(2)}, u32[]{:S(2)}) async-start(bf16[128,5,256]{2,1,0:T(8,128)(2,1)} %down.1), calls=%async_computation.8 | async-start | bytes 1048576 | tf_op jit(solution)/shard_map/all_to_all | solution.py:349
  280.2 19.1 %all-to-all-done.8 = bf16[128,5,256]{2,1,0:T(8,128)(2,1)S(1)} async-done(((bf16[128,5,256]{2,1,0:T(8,128)(2,1)}), bf16[128,5,256]{2,1,0:T(8,128)(2,1)S(1)}, u32[]{:S(2)}, u32[]{:S(2)}) %all-to-all-start.8) | async-done | bytes 327712 | tf_op jit(solution)/shard_map/all_to_all | solution.py:349
  (82 shorter events, 35.1 us)
Async XLA Ops:
  26.6 5.6 %copy-start.14 = (bf16[512,128]{1,0:T(8,128)(2,1)S(1)}, bf16[512,128]{1,0:T(8,128)(2,1)}, u32[]{:S(2)}) copy-start(bf16[512,128]{1,0:T(8,128)(2,1)} %param.14) | copy-start | bytes 393220
  27.9 18.2 %all-to-all-start.1 = ((bf16[4,576,256]{2,1,0:T(8,128)(2,1)}), bf16[4,576,256]{2,1,0:T(8,128)(2,1)S(1)}, u32[]{:S(2)}, u32[]{:S(2)}) async-start(bf16[4,576,256]{2,1,0:T(8,128)(2,1)} %broadcast_in_dim.19), calls=%async_computation.1 | async-start | bytes 2359296 | tf_op jit(solution)/shard_map/all_to_all | solution.py:273
  32.2 48.4 %all-gather.2.cloned.1.call-start = ((), (), s32[]{:S(2)}) async-start(), calls=%async_computation.9 | async-start | bytes 1179648 | tf_op jit(solution)/shard_map/all_gather | solution.py:290
  32.2 6.3 %collective-permute-start.1 = (bf16[512,128]{1,0:T(8,128)(2,1)S(1)}, bf16[512,128]{1,0:T(8,128)(2,1)S(1)}, u32[]{:S(2)}, u32[]{:S(2)}) collective-permute-start(bf16[512,128]{1,0:T(8,128)(2,1)S(1)} %copy-done.14), channel_id=1, source_target_pairs={{0,0},{1,64},{2,2},{3,66},{4,4},{5,68},{6,6},{7,70},{8,8},{9,72},{... | collective-permute-start | bytes 393224 | tf_op jit(solution)/shard_map/ppermute | solution.py:289
  46.1 4.7 %collective-permute-start = (bf16[4,576,256]{2,1,0:T(8,128)(2,1)S(1)}, bf16[4,576,256]{2,1,0:T(8,128)(2,1)S(1)}, u32[]{:S(2)}, u32[]{:S(2)}) collective-permute-start(bf16[4,576,256]{2,1,0:T(8,128)(2,1)S(1)} %all-to-all-done.1.own_ref), channel_id=1, source_target_pairs={{0,1},{1,0},{2,3},{3,2},{4,5},{5,4},{6,7},{7,6},{8,9},{9,8},{10,11... | collective-permute-start | bytes 3538952 | tf_op jit(solution)/shard_map/ppermute | solution.py:303
  56.7 37.4 %copy-start.8 = (bf16[1,4096,128]{2,1,0:T(8,128)(2,1)S(1)}, bf16[1,4096,128]{2,1,0:T(8,128)(2,1)}, u32[]{:S(2)}) copy-start(bf16[1,4096,128]{2,1,0:T(8,128)(2,1)} %param.18) | copy-start | bytes 3145732
  56.7 23.9 %all-to-all-start.2 = ((bf16[8,64,512]{2,1,0:T(8,128)(2,1)}), bf16[8,64,512]{2,1,0:T(8,128)(2,1)S(1)}, u32[]{:S(2)}, u32[]{:S(2)}) async-start(bf16[8,64,512]{2,1,0:T(8,128)(2,1)} %attend.1), calls=%async_computation.2 | async-start | bytes 1048576 | tf_op jit(solution)/shard_map/all_to_all | solution.py:308
  83.9 22.4 %all-to-all-start.3 = ((bf16[32,32,128]{2,1,0:T(8,128)(2,1)}), bf16[32,32,128]{2,1,0:T(8,128)(2,1)S(1)}, u32[]{:S(2)}, u32[]{:S(2)}) async-start(bf16[32,32,128]{2,1,0:T(8,128)(2,1)} %project.1), calls=%async_computation.3 | async-start | bytes 524288 | tf_op jit(solution)/shard_map/all_to_all | solution.py:312
  94.1 5.2 %copy-start.11 = (bf16[64,256]{1,0:T(8,128)(2,1)S(1)}, bf16[64,256]{1,0:T(8,128)(2,1)}, u32[]{:S(2)}) copy-start(bf16[64,256]{1,0:T(8,128)(2,1)} %param.10) | copy-start | bytes 98308
  94.1 5.2 %copy-start.12 = (s32[64,8]{0,1:T(8,128)S(1)}, s32[64,8]{0,1:T(8,128)}, u32[]{:S(2)}) copy-start(s32[64,8]{0,1:T(8,128)} %param.15) | copy-start | bytes 6148
  95.6 65.8 %copy-start.1 = (bf16[4096,256]{1,0:T(8,128)(2,1)}, bf16[4096,256]{1,0:T(8,128)(2,1)S(1)}, u32[]{:S(2)}) copy-start(bf16[4096,256]{1,0:T(8,128)(2,1)S(1)} %pad_maximum_fusion.refs_0_) | copy-start | bytes 6291460
  95.6 67.7 %collective-permute-start.3 = (bf16[4096,256]{1,0:T(8,128)(2,1)S(1)}, bf16[4096,256]{1,0:T(8,128)(2,1)}, u32[]{:S(2)}, u32[]{:S(2)}) collective-permute-start(bf16[4096,256]{1,0:T(8,128)(2,1)S(1)} %pad_maximum_fusion.refs_0_), channel_id=1, source_target_pairs={{0,2},{1,3},{2,0},{3,1},{4,6},{5,7},{6,4},{7,5},{8,10},{9,11},{10,... | collective-permute-start | bytes 6291464 | tf_op jit(solution)/shard_map/ppermute | solution.py:297
  107.2 40.9 %all-to-all-start.4 = ((f32[4,8,32,128]{3,2,1,0:T(8,128)}), f32[4,8,32,128]{3,2,1,0:T(8,128)S(1)}, u32[]{:S(2)}, u32[]{:S(2)}) async-start(f32[4,8,32,128]{3,2,1,0:T(8,128)} %broadcast_in_dim.20), calls=%async_computation.4 | async-start | bytes 1048576 | tf_op jit(solution)/shard_map/all_to_all | solution.py:273
  153.2 20.1 %all-to-all-start.5 = ((bf16[32,40,128]{2,1,0:T(8,128)(2,1)}), bf16[32,40,128]{2,1,0:T(8,128)(2,1)S(1)}, u32[]{:S(2)}, u32[]{:S(2)}) async-start(bf16[32,40,128]{2,1,0:T(8,128)(2,1)} %reshape.97), calls=%async_computation.5 | async-start | bytes 655360 | tf_op jit(solution)/shard_map/all_to_all | solution.py:343
  161.4 70.3 %collective-permute-start.2 = (bf16[4096,256]{1,0:T(8,128)(2,1)S(1)}, bf16[4096,256]{1,0:T(8,128)(2,1)}, u32[]{:S(2)}, u32[]{:S(2)}) collective-permute-start(bf16[4096,256]{1,0:T(8,128)(2,1)S(1)} %pad_maximum_fusion.refs_0_), channel_id=1, source_target_pairs={{0,1},{1,0},{2,3},{3,2},{4,5},{5,4},{6,7},{7,6},{8,9},{9,8},{10,11... | collective-permute-start | bytes 6291464 | tf_op jit(solution)/shard_map/ppermute | solution.py:279
  163.3 68.4 %collective-permute-start.4 = (bf16[4096,256]{1,0:T(8,128)(2,1)}, bf16[4096,256]{1,0:T(8,128)(2,1)}, u32[]{:S(2)}, u32[]{:S(2)}) collective-permute-start(bf16[4096,256]{1,0:T(8,128)(2,1)} %collective-permute-done.3.refs_2_), channel_id=1, source_target_pairs={{0,1},{1,0},{2,3},{3,2},{4,5},{5,4},{6,7},{7,6},{8,9},{9,8},{10,11... | collective-permute-start | bytes 6291464 | tf_op jit(solution)/shard_map/ppermute | solution.py:280
  174.8 57.0 %all-to-all-start.6 = ((bf16[4,160,1024]{2,1,0:T(8,128)(2,1)}), bf16[4,160,1024]{2,1,0:T(8,128)(2,1)S(1)}, u32[]{:S(2)}, u32[]{:S(2)}) async-start(bf16[4,160,1024]{2,1,0:T(8,128)(2,1)} %broadcast_in_dim.48), calls=%async_computation.6 | async-start | bytes 2621440 | tf_op jit(solution)/shard_map/all_to_all | solution.py:273
  181.4 48.4 %collective-permute-start.6 = (bf16[2048,256]{1,0:T(8,128)(2,1)}, bf16[2048,256]{1,0:T(8,128)(2,1)}, u32[]{:S(2)}, u32[]{:S(2)}) collective-permute-start(bf16[2048,256]{1,0:T(8,128)(2,1)} %bitcast.44), channel_id=1, source_target_pairs={{0,2},{1,3},{2,0},{3,1},{4,6},{5,7},{6,4},{7,5},{8,10},{9,11},{10,... | collective-permute-start | bytes 3145736 | tf_op jit(solution)/shard_map/ppermute | solution.py:298
  183.9 62.3 %collective-permute-start.5 = (bf16[2048,256]{1,0:T(8,128)(2,1)}, bf16[2048,256]{1,0:T(8,128)(2,1)}, u32[]{:S(2)}, u32[]{:S(2)}) collective-permute-start(bf16[2048,256]{1,0:T(8,128)(2,1)} %bitcast.45), channel_id=1, source_target_pairs={{0,1},{1,0},{2,3},{3,2},{4,5},{5,4},{6,7},{7,6},{8,9},{9,8},{10,11... | collective-permute-start | bytes 3145736 | tf_op jit(solution)/shard_map/ppermute | solution.py:279
  229.8 16.4 %collective-permute-start.7 = (bf16[2048,256]{1,0:T(8,128)(2,1)}, bf16[2048,256]{1,0:T(8,128)(2,1)}, u32[]{:S(2)}, u32[]{:S(2)}) collective-permute-start(bf16[2048,256]{1,0:T(8,128)(2,1)} %collective-permute-done.6.refs_2_), channel_id=1, source_target_pairs={{0,1},{1,0},{2,3},{3,2},{4,5},{5,4},{6,7},{7,6},{8,9},{9,8},{10,11... | collective-permute-start | bytes 3145736 | tf_op jit(solution)/shard_map/ppermute | solution.py:280
  239.3 27.0 %all-to-all-start.7 = ((bf16[4,160,512]{2,1,0:T(8,128)(2,1)}), bf16[4,160,512]{2,1,0:T(8,128)(2,1)S(1)}, u32[]{:S(2)}, u32[]{:S(2)}) async-start(bf16[4,160,512]{2,1,0:T(8,128)(2,1)} %hidden.1), calls=%async_computation.7 | async-start | bytes 1310720 | tf_op jit(solution)/shard_map/all_to_all | solution.py:347
  246.2 33.4 %copy-start.13 = (f32[64,8]{0,1:T(8,128)S(1)}, f32[64,8]{0,1:T(8,128)}, u32[]{:S(2)}) copy-start(f32[64,8]{0,1:T(8,128)} %param.16) | copy-start | bytes 6148
  271.8 27.6 %copy-start.10 = (bf16[64,256]{1,0:T(8,128)(2,1)S(1)}, bf16[64,256]{1,0:T(8,128)(2,1)}, u32[]{:S(2)}) copy-start(bf16[64,256]{1,0:T(8,128)(2,1)} %get-tuple-element.7) | copy-start | bytes 98308
  271.8 27.5 %all-to-all-start.8 = ((bf16[128,5,256]{2,1,0:T(8,128)(2,1)}), bf16[128,5,256]{2,1,0:T(8,128)(2,1)S(1)}, u32[]{:S(2)}, u32[]{:S(2)}) async-start(bf16[128,5,256]{2,1,0:T(8,128)(2,1)} %down.1), calls=%async_computation.8 | async-start | bytes 1048576 | tf_op jit(solution)/shard_map/all_to_all | solution.py:349
  (8 other events, 10.9 us)
Sparse Core Ops, SparseCore 0:
  39.3 41.2 all-gather.1
